TPU v7x, 256 devices: a whole 4x4x8 slice. The times are simulated.
256 devices in a mesh: sess: 16 (over z, core), tp: 16 (over y, x).
Axes of the slice: x: 4, y: 4, z: 8, core: 2. Of those that a mesh axis runs over, the one named last changes fastest.
Arguments:
- frames: bfloat16 [256, 4096], P('sess', 'tp'), may hold values from -6 to 6
- norm_gain: bfloat16 [4096], replicated, may hold values from 0.5 to 1.5
- w_qkv: bfloat16 [3, 4096, 2048], P(None, None, 'tp'), may hold values from -0.09375 to 0.09375
- w_out: bfloat16 [2048, 4096], P('tp'), may hold values from -0.5 to 0.5
- kv_cache: bfloat16 [2, 512, 375, 2048], P(None, 'sess', None, 'tp'), may hold values from -800 to 800
- frame_session: int32 [256], replicated, may hold values from 0 to 255, as said below
- owner_of: int32 [256], replicated, may hold values from 0 to 15, as said below
- context_len: int32 [256], replicated, may hold values from 1 to 375, as said below
Outputs:
- hidden_rows: bfloat16 [256, 4096], P('sess', 'tp')
Inputs may be any that keep to these rules, and one draw needn't show every extreme that they name: `frame_session`: a permutation of the sessions; at most 2 of the frame rows of one index of sess have the same owner, and some rows reach 2. `owner_of`: each owner holds at most 32 sessions, and some owner holds exactly 32. `context_len`: some session has exactly 375.
All inputs are finite; a program needn't handle non-finite values.
Results may differ from a plain program's by a relative error of at most 0.014.
The roundings to bfloat16 on the way count: a program that leaves them out, or rounds other values in their place, can miss the bound.
Values may be sent and summed in bfloat16 or wider, within the bound.
No kernel may reach another device: no remote copies, remote signals or barrier semaphores. Data moves between devices by JAX's collectives and lax.ppermute only.
A program may use at most 64 MiB of HBM per device.

v0:
```python
import jax
import jax.numpy as jnp
from jax import lax
from jax.sharding import PartitionSpec as P

HD = 128


def laid_out(tiles, dim):
    tiles = jnp.moveaxis(tiles, 0, dim)
    shape = tiles.shape
    return tiles.reshape(*shape[:dim], shape[dim] * shape[dim + 1], *shape[dim + 2 :])


def sent_to_all(array, axis):
    copies = jnp.broadcast_to(array, (lax.axis_size(axis), *array.shape))
    return lax.all_to_all(copies, axis, split_axis=0, concat_axis=0, tiled=True)


def gathered_copies(array, axis, dim):
    return laid_out(sent_to_all(array, axis), dim)


def split_up(array, dim, peers):
    before, after = (array.shape[:dim], array.shape[dim + 1 :])
    return jnp.moveaxis(array.reshape(*before, peers, -1, *after), dim, 0)


def sum_at_owner(array, axis, dim):
    tiles = split_up(array, dim, lax.axis_size(axis))
    arrived = lax.all_to_all(tiles, axis, split_axis=0, concat_axis=0, tiled=True)
    return arrived.astype(jnp.float32).sum(axis=0)


def attend_slots(gathered, kv_cache, slot_length, head_size):
    slot_count = gathered.shape[0]
    head_cols = gathered.shape[2]
    heads_count = head_cols // head_size
    context = kv_cache.shape[2]
    queries = gathered[:, 0].reshape(slot_count, heads_count, head_size)
    new_keys = gathered[:, 1].reshape(slot_count, heads_count, head_size)
    new_values = gathered[:, 2].reshape(slot_count, heads_count, head_size)
    cached_keys = kv_cache[0].reshape(slot_count, context, heads_count, head_size)
    cached_values = kv_cache[1].reshape(slot_count, context, heads_count, head_size)
    factor = 1.0 / jnp.sqrt(jnp.float32(head_size))
    scores = (
        jnp.einsum("shd,sthd->sht", queries, cached_keys, preferred_element_type=jnp.float32)
        * factor
    )
    own_score = (
        jnp.sum(queries.astype(jnp.float32) * new_keys.astype(jnp.float32), axis=-1) * factor
    )
    valid = jnp.arange(context, dtype=jnp.int32)[None, None, :] < slot_length[:, None, None]
    scores = jnp.where(valid, scores, -jnp.inf)
    top_score = jnp.maximum(jnp.max(scores, axis=-1), own_score)
    expo = jnp.where(valid, jnp.exp(scores - top_score[..., None]), 0.0)
    own_exp = jnp.exp(own_score - top_score)
    total = jnp.sum(expo, axis=-1) + own_exp
    weights = (expo / total[..., None]).astype(jnp.bfloat16)
    own_weight = (own_exp / total).astype(jnp.bfloat16)
    mixed = jnp.einsum("sht,sthd->shd", weights, cached_values, preferred_element_type=jnp.float32)
    mixed = mixed + own_weight.astype(jnp.float32)[..., None] * new_values.astype(jnp.float32)
    return mixed.astype(jnp.bfloat16).reshape(slot_count, head_cols)


def body(frames, norm_gain, w_qkv, w_out, kv_cache, frame_session, owner_of, context_len):
    sess_count = lax.axis_size("sess")
    owner_index = lax.axis_index("sess")
    rows_local = frames.shape[0]
    slot_count = kv_cache.shape[1]
    head_cols = w_qkv.shape[2]
    sessions = frame_session.shape[0]
    pair_cap = (slot_count + sess_count - 1) // sess_count
    position_count = sess_count * pair_cap
    whole = gathered_copies(frames, "tp", 1)
    wide = whole.astype(jnp.float32)
    normed = (
        wide
        * lax.rsqrt(jnp.mean(wide * wide, axis=1, keepdims=True) + 1e-05)
        * norm_gain.astype(jnp.float32)
    ).astype(jnp.bfloat16)
    projected = jnp.einsum("rd,cde->rce", normed, w_qkv, preferred_element_type=jnp.float32).astype(
        jnp.bfloat16
    )
    projected = projected.reshape(rows_local, 3 * head_cols)
    session_ids = jnp.arange(sessions, dtype=jnp.int32)
    same_owner = owner_of[:, None] == owner_of[None, :]
    slot_of = jnp.sum(same_owner & (session_ids[None, :] < session_ids[:, None]), axis=1)
    matches = frame_session[:, None] == session_ids[None, :]
    row_owner = jnp.sum(jnp.where(matches, owner_of[None, :], 0), axis=1)
    row_slot = jnp.sum(jnp.where(matches, slot_of[None, :], 0), axis=1)
    row_length = jnp.sum(jnp.where(matches, context_len[None, :], 0), axis=1)
    row_block = session_ids // rows_local
    row_same = (row_owner[:, None] == row_owner[None, :]) & (
        row_block[:, None] == row_block[None, :]
    )
    row_pair = jnp.sum(row_same & (session_ids[None, :] < session_ids[:, None]), axis=1)
    row_target = row_block * pair_cap + row_pair
    send_target = row_owner * pair_cap + row_pair
    local_target = lax.dynamic_slice_in_dim(send_target, owner_index * rows_local, rows_local)
    position_ids = jnp.arange(position_count, dtype=jnp.int32)
    dispatch = (position_ids[:, None] == local_target[None, :]).astype(jnp.bfloat16)
    outgoing = jnp.dot(dispatch, projected, preferred_element_type=jnp.float32).astype(jnp.bfloat16)
    outgoing = outgoing.reshape(sess_count, pair_cap, 3 * head_cols)
    incoming = lax.all_to_all(outgoing, "sess", split_axis=0, concat_axis=0, tiled=True).reshape(
        position_count, 3 * head_cols
    )
    owned = row_owner == owner_index
    slot_ids = jnp.arange(slot_count, dtype=jnp.int32)
    slot_rows = (row_slot[None, :] == slot_ids[:, None]) & owned[None, :]
    row_place = row_target[:, None] == position_ids[None, :]
    collect = jnp.dot(slot_rows.astype(jnp.float32), row_place.astype(jnp.float32)).astype(
        jnp.bfloat16
    )
    slot_length = jnp.sum(jnp.where(slot_rows, row_length[None, :], 0), axis=1)
    gathered = jnp.dot(collect, incoming, preferred_element_type=jnp.float32).astype(jnp.bfloat16)
    gathered = gathered.reshape(slot_count, 3, head_cols)
    attended = attend_slots(gathered, kv_cache, slot_length, HD)
    returned = jnp.dot(collect.T, attended, preferred_element_type=jnp.float32).astype(jnp.bfloat16)
    returned = returned.reshape(sess_count, pair_cap, head_cols)
    arrived = lax.all_to_all(returned, "sess", split_axis=0, concat_axis=0, tiled=True).reshape(
        position_count, head_cols
    )
    regrouped = jnp.dot(dispatch.T, arrived, preferred_element_type=jnp.float32).astype(
        jnp.bfloat16
    )
    partial_rows = jnp.dot(regrouped, w_out, preferred_element_type=jnp.float32)
    branch = sum_at_owner(partial_rows.astype(jnp.bfloat16), "tp", 1)
    return (frames.astype(jnp.float32) + branch).astype(jnp.bfloat16)


def solution(mesh):
    in_specs = (
        P("sess", "tp"),
        P(),
        P(None, None, "tp"),
        P("tp", None),
        P(None, "sess", None, "tp"),
        P(),
        P(),
        P(),
    )
    out_specs = P("sess", "tp")
    return jax.shard_map(body, mesh=mesh, in_specs=in_specs, out_specs=out_specs, check_vma=False)
```

profile of v0, /device:TPU:1, one launch (start us, length us, event | category | flops | bytes accessed | tf_op | source)
XLA Modules:
  0.0 69.8 jit_solution(9968431946873528415)
XLA Ops:
  0.0 0.0 copy-start
  0.0 1.5 %broadcast_in_dim.82 = bf16[16,16,256]{2,1,0:T(8,128)(2,1)} broadcast(bf16[16,256]{1,0:T(8,128)(2,1)} %param.8), dimensions={1,2} | broadcast | bytes 139264 | tf_op jit(solution)/shard_map/broadcast_in_dim | solution.py:16
  1.5 7.6 %all-to-all-start = ((bf16[16,16,256]{2,1,0:T(8,128)(2,1)}), bf16[16,16,256]{2,1,0:T(8,128)(2,1)S(1)}, u32[]{:S(2)}, u32[]{:S(2)}) async-start(bf16[16,16,256]{2,1,0:T(8,128)(2,1)} %broadcast_in_dim.82), calls=%async_computation | async-start | bytes 262144 | tf_op jit(solution)/shard_map/all_to_all | solution.py:17
  9.1 0.9 %convert_reduce_fusion.1 = s32[256]{0:T(256)S(1)} fusion(s32[256]{0:T(256)} %param.14), kind=kLoop, calls=%fused_computation.23 | loop fusion | flops 327424 | bytes 2048 | tf_op jit(solution)/shard_map/reduce_sum | solution.py:88
  10.0 1.0 %select_reduce_fusion = (s32[256]{0:T(256)S(1)}, s32[256]{0:T(256)S(1)}, s32[256]{0:T(256)S(1)}) fusion(s32[256]{0:T(256)} %param.15, s32[256]{0:T(256)} %param.13, s32[256]{0:T(256)S(1)} %convert_reduce_fusion.1, s32[256]{0:T(256)} %param.14), kind=kLoop, calls=%fused_computation.21 | loop fusion | flops 457984 | bytes 7168 | tf_op jit(solution)/shard_map/reduce_sum | solution.py:92
  11.1 0.2 convert_reduce_fusion.2
  11.3 0.7 %convert_element_type.100 = f32[4096]{0:T(1024)S(1)} convert(bf16[4096]{0:T(1024)(128)(2,1)} %param.9) | non-fusion elementwise | flops 4096 | bytes 24576 | tf_op jit(solution)/shard_map/convert_element_type | solution.py:80
  12.0 6.5 %slice_bitcast_fusion.1 = (bf16[32,375,128]{2,0,1:T(8,128)(2,1)}, bf16[32,375,128]{2,0,1:T(8,128)(2,1)}) fusion(bf16[2,32,375,128]{3,1,2,0:T(8,128)(2,1)} %param.12), kind=kLoop, calls=%fused_computation.6 | loop fusion | bytes 12288000 | tf_op jit(solution)/shard_map/reshape.3
  18.4 0.1 dynamic_slice.3
  18.5 0.2 convolution_convert_fusion.5
  18.7 0.0 all-to-all-done
  18.7 0.2 fusion.11
  19.0 0.0 copy-done
  19.0 0.6 fusion.10
  19.5 0.1 convolution_convert_fusion.2
  19.7 0.6 reshape.161
  20.3 9.4 %all-to-all-start.1 = ((bf16[16,2,384]{2,1,0:T(2,128)(2,1)}), bf16[16,2,384]{2,1,0:T(2,128)(2,1)S(1)}, u32[]{:S(2)}, u32[]{:S(2)}) async-start(bf16[16,2,384]{2,1,0:T(2,128)(2,1)} %reshape.161), calls=%async_computation.1 | async-start | bytes 49152 | tf_op jit(solution)/shard_map/all_to_all | solution.py:105
  29.7 0.1 select_reduce_fusion.3
  29.8 7.2 %all-to-all-done.1 = bf16[16,2,384]{2,1,0:T(2,128)(2,1)S(1)} async-done(((bf16[16,2,384]{2,1,0:T(2,128)(2,1)}), bf16[16,2,384]{2,1,0:T(2,128)(2,1)S(1)}, u32[]{:S(2)}, u32[]{:S(2)}) %all-to-all-start.1) | async-done | bytes 24608 | tf_op jit(solution)/shard_map/all_to_all | solution.py:105
  37.1 0.1 convolution_convert_fusion.1
  37.2 0.0 copy-start.1
  37.2 0.3 fusion.30
  37.6 3.7 %fusion.2 = f32[32,1,375]{2,1,0:T(1,128)S(1)} fusion(bf16[32,375,128]{2,0,1:T(8,128)(2,1)} %get-tuple-element.8, bf16[32,3,128]{2,1,0:T(4,128)(2,1)S(1)} %reshape.163), kind=kOutput, calls=%fused_computation.3 | convolution fusion | flops 3072000 | bytes 3136384 | tf_op jit(solution)/shard_map/shd,sthd->sht/dot_general | solution.py:47
  41.2 0.0 copy-start.2
  41.2 0.2 fusion.24
  41.5 0.2 fusion.21
  41.7 0.1 fusion.25
  41.8 0.0 copy-done.1
  41.8 2.1 %fusion.7 = bf16[32,1,128]{2,1,0:T(2,128)(2,1)S(1)} fusion(bf16[32,375,128]{2,0,1:T(8,128)(2,1)S(1)} %copy-done.1, bf16[32,375,1]{1,0,2:T(8,128)(2,1)S(1)} %fusion.25, bf16[32,3,128]{2,1,0:T(4,128)(2,1)S(1)} %reshape.163, f32[32]{0:T(128)S(1)} %get-tuple-element.10), kind=kOutput, calls=%fused_computation.11 | convolution fusion | flops 3088384 | bytes 3112512 | tf_op jit(solution)/shard_map/sht,sthd->shd/dot_general | solution.py:61
  43.9 0.2 convolution_convert_fusion.4
  44.1 9.9 %all_to_all.20 = bf16[16,2,128]{2,1,0:T(2,128)(2,1)S(1)} all-to-all(bf16[16,2,128]{2,1,0:T(2,128)(2,1)S(1)} %bitcast.57), channel_id=1, replica_groups=mesh['sess'=16,'tp'=16] {'sess'}, dimensions={0} | all-to-all | bytes 16384 | tf_op jit(solution)/shard_map/all_to_all | solution.py:121
  54.0 1.6 %convolution_convert_fusion = bf16[16,4096]{1,0:T(8,128)(2,1)S(1)} fusion(bf16[128,4096]{1,0:T(8,128)(2,1)} %param.11, bf16[32,128]{1,0:T(8,128)(2,1)S(1)} %bitcast.56, s32[16]{0:T(128)S(1)} %dynamic_slice.3), kind=kOutput, calls=%fused_computation | convolution fusion | flops 16976384 | bytes 1187904 | tf_op jit(solution)/shard_map/dot_general | solution.py:127
  55.6 13.6 %all_to_all.21 = bf16[16,16,256]{2,1,0:T(8,128)(2,1)S(1)} all-to-all(bf16[16,16,256]{2,1,0:T(8,128)(2,1)S(1)} %bitcast.55), channel_id=1, replica_groups=mesh['sess'=16,'tp'=16] {'tp'}, dimensions={0} | all-to-all | bytes 262144 | tf_op jit(solution)/shard_map/all_to_all | solution.py:31
  69.2 0.0 copy-done.2
  69.2 0.6 add_convert_fusion
  (12 shorter events, 0.2 us)
Async XLA Ops:
  0.0 19.0 %copy-start = (bf16[3,4096,128]{2,1,0:T(8,128)(2,1)S(1)}, bf16[3,4096,128]{2,1,0:T(8,128)(2,1)}, u32[]{:S(2)}) copy-start(bf16[3,4096,128]{2,1,0:T(8,128)(2,1)} %param.10) | copy-start | bytes 9437188
  1.5 17.2 %all-to-all-start = ((bf16[16,16,256]{2,1,0:T(8,128)(2,1)}), bf16[16,16,256]{2,1,0:T(8,128)(2,1)S(1)}, u32[]{:S(2)}, u32[]{:S(2)}) async-start(bf16[16,16,256]{2,1,0:T(8,128)(2,1)} %broadcast_in_dim.82), calls=%async_computation | async-start | bytes 262144 | tf_op jit(solution)/shard_map/all_to_all | solution.py:17
  20.3 16.8 %all-to-all-start.1 = ((bf16[16,2,384]{2,1,0:T(2,128)(2,1)}), bf16[16,2,384]{2,1,0:T(2,128)(2,1)S(1)}, u32[]{:S(2)}, u32[]{:S(2)}) async-start(bf16[16,2,384]{2,1,0:T(2,128)(2,1)} %reshape.161), calls=%async_computation.1 | async-start | bytes 49152 | tf_op jit(solution)/shard_map/all_to_all | solution.py:105
  37.2 4.6 %copy-start.1 = (bf16[32,375,128]{2,0,1:T(8,128)(2,1)S(1)}, bf16[32,375,128]{2,0,1:T(8,128)(2,1)}, u32[]{:S(2)}) copy-start(bf16[32,375,128]{2,0,1:T(8,128)(2,1)} %get-tuple-element.9) | copy-start | bytes 9216004
  41.2 28.0 %copy-start.2 = (bf16[16,256]{1,0:T(8,128)(2,1)S(1)}, bf16[16,256]{1,0:T(8,128)(2,1)}, u32[]{:S(2)}) copy-start(bf16[16,256]{1,0:T(8,128)(2,1)} %param.8) | copy-start | bytes 24580
where the time goes:
time: 70.3 us; the launch traced here: 69.8 us
  blocking collectives  23.5 us (33%)
  starting transfers between devices  17 us (24%)
  local copies, waits for them, and re-layouts  8.74 us (12%)
  matrix products  8.65 us (12%)
  waiting for transfers between devices  7.22 us (10%)
  other arithmetic  4.63 us (7%)
    all_to_all x1, blocking collectives, sum_at_owner(): lax.all_to_all(tiles, axis, split_axis=0, concat_axis=0, tiled=True)  13.6 us
    all_to_all x1, blocking collectives, body(): lax.all_to_all(returned, 'sess', split_axis=0, concat_axis=0, tiled=True)  9.86 us
    all_to_all x1, starting transfers between devices, body(): lax.all_to_all(outgoing, 'sess', split_axis=0, concat_axis=0, tiled=True)  9.43 us
    all_to_all x1, starting transfers between devices, sent_to_all(): return lax.all_to_all(copies, axis, split_axis=0, concat_axis=0, tiled=True)  7.57 us
    all_to_all x1, waiting for transfers between devices, body(): lax.all_to_all(outgoing, 'sess', split_axis=0, concat_axis=0, tiled=True)  7.21 us
    another operation x1, local copies, waits for them, and re-layouts  6.46 us
    dot_general x1, matrix products, attend_slots(): jnp.einsum('shd,sthd->sht', queries, cached_keys, preferred_element_type=...  3.69 us
    dot_general x1, matrix products, attend_slots(): jnp.einsum('sht,sthd->shd', weights, cached_values, preferred_element_typ...  2.13 us
  transfers between devices with their start and end apart: 2, of which 1 were waited for; matrix products, arithmetic and copies ran while one was open for 14% of the time, Pallas kernels for 0%

commit v1 on v0

v1 whole, which is shorter than its diff:
```python
import jax
import jax.numpy as jnp
from jax import lax
from jax.experimental import pallas as pl
from jax.experimental.pallas import tpu as pltpu
from jax.sharding import PartitionSpec as P

HD = 128
BF = jnp.bfloat16
F32 = jnp.float32
VM = pl.BlockSpec(memory_space=pltpu.VMEM)
SM = pl.BlockSpec(memory_space=pltpu.SMEM)


def row_targets(session_ref, owner_ref, block, rows, cap, count_ref, owners):
    for o in range(owners):
        count_ref[o] = 0
    targets = []
    for r in range(rows):
        o = owner_ref[session_ref[block * rows + r]]
        pair = count_ref[o]
        count_ref[o] = pair + 1
        targets.append(o * cap + pair)
    return targets


def dispatch_kernel(block_ref, session_ref, owner_ref, frames_ref, out_ref, held, count_ref):
    rows = frames_ref.shape[0]
    owners, peers, cap, width = out_ref.shape
    held[...] = jnp.zeros_like(held)
    wide = frames_ref[...].astype(F32)
    targets = row_targets(session_ref, owner_ref, block_ref[0], rows, cap, count_ref, owners)
    for r in range(rows):
        held[pl.ds(targets[r], 1), :] = wide[r : r + 1]
    for o in range(owners):
        pair = held[o * cap : (o + 1) * cap, :].astype(BF)
        out_ref[o] = jnp.broadcast_to(pair[None], (peers, cap, width))


def attend_kernel(
    x_ref, gain_ref, w_ref, kv_ref, w_out_ref, collect_ref, place_ref, length_ref,
    out_ref, rows_ref, score_ref, spread_ref,
):
    owners, peers, cap, width = x_ref.shape
    places = owners * cap
    model = peers * width
    context, slots = kv_ref.shape[1], kv_ref.shape[2]
    group = HD // slots
    steps = (context + group) // group
    for s in range(owners):
        for t in range(peers):
            rows_ref[s * cap : (s + 1) * cap, t * width : (t + 1) * width] = x_ref[s, t]
    wide = rows_ref[...].astype(F32)
    scale = lax.rsqrt(jnp.sum(wide * wide, axis=1, keepdims=True) / model + 1e-05)
    normed = (wide * scale * gain_ref[...]).astype(BF)
    projected = [
        jnp.dot(normed, w_ref[c], preferred_element_type=F32).astype(BF) for c in range(3)
    ]
    collect = collect_ref[...]
    query, new_key, new_value = [
        jnp.dot(collect, p, preferred_element_type=F32).astype(BF) for p in projected
    ]
    lane = lax.broadcasted_iota(jnp.int32, (slots, HD), 1)
    own = lax.broadcasted_iota(jnp.int32, (slots, HD), 0) == lane % slots
    for g in range(steps):
        if g < steps - 1:
            keys = kv_ref[0, g * group : (g + 1) * group].reshape(HD, HD)
        else:
            tail = kv_ref[0, g * group : context].reshape(HD - slots, HD)
            keys = jnp.concatenate([tail, new_key], axis=0)
        dots = lax.dot_general(
            query, keys, (((1,), (1,)), ((), ())), preferred_element_type=F32
        )
        score_ref[g : g + 1, :] = jnp.sum(jnp.where(own, dots, 0.0), axis=0, keepdims=True)
    scores = score_ref[0:steps, :] * (1.0 / jnp.sqrt(F32(HD)))
    lanes = lax.broadcasted_iota(jnp.int32, (steps, HD), 1)
    frame = lax.broadcasted_iota(jnp.int32, (steps, HD), 0) * group + lanes // slots
    valid = (frame < length_ref[...]) | (frame == context)
    scores = jnp.where(valid, scores, -jnp.inf)
    top = jnp.max(scores, axis=0, keepdims=True)
    shift = slots
    while shift < HD:
        top = jnp.maximum(top, pltpu.roll(top, shift, 1))
        shift *= 2
    expo = jnp.where(valid, jnp.exp(scores - top), 0.0)
    total = jnp.sum(expo, axis=0, keepdims=True)
    shift = slots
    while shift < HD:
        total = total + pltpu.roll(total, shift, 1)
        shift *= 2
    score_ref[0:steps, :] = expo / total
    place = place_ref[...] > 0.0
    mixed = jnp.zeros((places, HD), F32)
    for g in range(steps):
        weights = jnp.where(place, score_ref[g : g + 1, :], 0.0).astype(BF)
        if g < steps - 1:
            values = kv_ref[1, g * group : (g + 1) * group].reshape(HD, HD)
        else:
            tail = kv_ref[1, g * group : context].reshape(HD - slots, HD)
            values = jnp.concatenate([tail, new_value], axis=0)
        mixed += jnp.dot(weights, values, preferred_element_type=F32)
    attended = mixed.astype(BF)
    for t in range(peers):
        part = jnp.dot(
            attended, w_out_ref[:, t * width : (t + 1) * width], preferred_element_type=F32
        ).astype(BF)
        for s in range(owners):
            out_ref[s, t] = part[s * cap : (s + 1) * cap]


def finish_kernel(block_ref, session_ref, owner_ref, parts_ref, frames_ref, out_ref, held, sums, count_ref):
    rows = frames_ref.shape[0]
    owners, peers, cap, width = parts_ref.shape
    targets = row_targets(session_ref, owner_ref, block_ref[0], rows, cap, count_ref, owners)
    for o in range(owners):
        held[o * cap : (o + 1) * cap, :] = jnp.sum(parts_ref[o].astype(F32), axis=0)
    for r in range(rows):
        sums[r : r + 1, :] = held[pl.ds(targets[r], 1), :]
    out_ref[...] = (frames_ref[...].astype(F32) + sums[...]).astype(BF)


def body(frames, norm_gain, w_qkv, w_out, kv_cache, frame_session, owner_of, context_len):
    owners = lax.axis_size("sess")
    peers = lax.axis_size("tp")
    me = lax.axis_index("sess")
    rows, width = frames.shape
    slots = kv_cache.shape[1]
    sessions = frame_session.shape[0]
    cap = (slots + owners - 1) // owners
    places = owners * cap
    block = me.reshape(1).astype(jnp.int32)
    exchange = (owners, peers, cap, width)

    outgoing = pl.pallas_call(
        dispatch_kernel,
        out_shape=jax.ShapeDtypeStruct(exchange, BF),
        in_specs=[SM, SM, SM, VM],
        out_specs=VM,
        scratch_shapes=[pltpu.VMEM((places, width), F32), pltpu.SMEM((owners,), jnp.int32)],
        name="dispatch",
    )(block, frame_session, owner_of, frames)
    arrived = lax.all_to_all(
        outgoing.reshape(owners * peers, cap, width),
        ("sess", "tp"), split_axis=0, concat_axis=0, tiled=True,
    ).reshape(exchange)

    session_ids = jnp.arange(sessions, dtype=jnp.int32)
    mine = owner_of == me
    slot_of = jnp.sum(mine[None, :] & (session_ids[None, :] < session_ids[:, None]), axis=1)
    matches = frame_session[:, None] == session_ids[None, :]
    row_mine = jnp.any(matches & mine[None, :], axis=1)
    row_slot = jnp.sum(jnp.where(matches, slot_of[None, :], 0), axis=1)
    row_block = session_ids // rows
    earlier = (row_block[:, None] == row_block[None, :]) & (session_ids[None, :] < session_ids[:, None])
    row_pair = jnp.sum(earlier & row_mine[None, :], axis=1)
    row_place = jnp.where(row_mine, row_block * cap + row_pair, -1)
    place_ids = jnp.arange(places, dtype=jnp.int32)
    at_place = row_place[None, :] == place_ids[:, None]
    place_slot = jnp.sum(jnp.where(at_place, row_slot[None, :] + 1, 0), axis=1) - 1
    slot_ids = jnp.arange(slots, dtype=jnp.int32)
    collect = (slot_ids[:, None] == place_slot[None, :]).astype(BF)
    lane_slot = jnp.arange(HD, dtype=jnp.int32) % slots
    place_mask = (place_slot[:, None] == lane_slot[None, :]).astype(F32)
    lane_session = mine[:, None] & (slot_of[:, None] == lane_slot[None, :])
    lengths = jnp.sum(jnp.where(lane_session, context_len[:, None], 0), axis=0)[None, :]

    context = kv_cache.shape[2]
    steps = (context + HD // slots) // (HD // slots)
    partial_rows = pl.pallas_call(
        attend_kernel,
        out_shape=jax.ShapeDtypeStruct(exchange, BF),
        in_specs=[VM] * 8,
        out_specs=VM,
        scratch_shapes=[
            pltpu.VMEM((places, peers * width), BF),
            pltpu.VMEM((steps + (-steps) % 8, HD), F32),
            pltpu.VMEM((8, HD), F32),
        ],
        name="attend",
    )(
        arrived,
        norm_gain.astype(F32).reshape(1, -1),
        w_qkv,
        kv_cache.transpose(0, 2, 1, 3),
        w_out,
        collect,
        place_mask,
        lengths,
    )
    parts = lax.all_to_all(
        partial_rows.reshape(owners * peers, cap, width),
        ("sess", "tp"), split_axis=0, concat_axis=0, tiled=True,
    ).reshape(exchange)
    return pl.pallas_call(
        finish_kernel,
        out_shape=jax.ShapeDtypeStruct(frames.shape, frames.dtype),
        in_specs=[SM, SM, SM, VM, VM],
        out_specs=VM,
        scratch_shapes=[
            pltpu.VMEM((places, width), F32),
            pltpu.VMEM((rows, width), F32),
            pltpu.SMEM((owners,), jnp.int32),
        ],
        name="finish",
    )(block, frame_session, owner_of, parts, frames)


def solution(mesh):
    in_specs = (
        P("sess", "tp"),
        P(),
        P(None, None, "tp"),
        P("tp", None),
        P(None, "sess", None, "tp"),
        P(),
        P(),
        P(),
    )
    out_specs = P("sess", "tp")
    return jax.shard_map(body, mesh=mesh, in_specs=in_specs, out_specs=out_specs, check_vma=False)
```

time: 70.3 us -> 67.9 us (0.966)
  Pallas kernels: 0 us -> 13.8 us
  matrix products: 8.65 us -> 0 us
  local copies, waits for them, and re-layouts: 8.74 us -> 0.7 us
  other arithmetic: 4.63 us -> 6.82 us
  blocking collectives: 23.5 us -> 21.7 us
  waiting for transfers between devices: 7.22 us -> 8.84 us
  starting transfers between devices: 17 us -> 15.7 us
    pallas_call x0 -> x3, Pallas kernels: none -> 13.8 us  [the longest x1 10.4 us: body(): pl.pallas_call(attend_kernel, out_shape=jax.ShapeDtypeStruct(exchange, BF...]
    dot_general x8 -> x0, matrix products: 8.65 us -> none  [the longest x1 3.69 us: attend_slots(): jnp.einsum('shd,sthd->sht', queries, cached_keys, preferred_element_type=...]
    another operation x1 -> x0, local copies, waits for them, and re-layouts: 6.46 us -> none
    all_to_all x2 -> x1, blocking collectives: 23.5 us -> 21.7 us  [body(): lax.all_to_all(partial_rows.reshape(owners * peers, cap, width), ('sess',...]
    all_to_all x2 -> x1, waiting for transfers between devices: 7.22 us -> 8.84 us  [body(): lax.all_to_all(outgoing.reshape(owners * peers, cap, width), ('sess', 'tp...]
    broadcast_in_dim x1 -> x0, local copies, waits for them, and re-layouts: 1.51 us -> none  [sent_to_all(): copies = jnp.broadcast_to(array, (lax.axis_size(axis), *array.shape))]
    all_to_all x2 -> x1, starting transfers between devices: 17 us -> 15.7 us  [body(): lax.all_to_all(outgoing.reshape(owners * peers, cap, width), ('sess', 'tp...]
    reshape x0 -> x1, other arithmetic: none -> 1.3 us  [body(): norm_gain.astype(F32).reshape(1, -1)]
  transfers between devices with their start and end apart: 2 -> 1, of which waited for: 1 -> 1; matrix products, arithmetic and copies ran while one was open for 14% -> 10% of each run, Pallas kernels for 0% -> 0%
where the time goes in v1:
time: 67.9 us; the launch traced here: 67.5 us
  blocking collectives  21.7 us (32%)
  starting transfers between devices  15.7 us (23%)
  Pallas kernels  13.8 us (20%)
  waiting for transfers between devices  8.84 us (13%)
  other arithmetic  6.82 us (10%)
  local copies, waits for them, and re-layouts  0.7 us (1%)
    all_to_all x1, blocking collectives, body(): lax.all_to_all(partial_rows.reshape(owners * peers, cap, width), ('sess',...  21.7 us
    all_to_all x1, starting transfers between devices, body(): lax.all_to_all(outgoing.reshape(owners * peers, cap, width), ('sess', 'tp...  15.7 us
    pallas_call x1, Pallas kernels, body(): pl.pallas_call(attend_kernel, out_shape=jax.ShapeDtypeStruct(exchange, BF...  10.4 us
    all_to_all x1, waiting for transfers between devices, body(): lax.all_to_all(outgoing.reshape(owners * peers, cap, width), ('sess', 'tp...  8.84 us
    pallas_call x1, Pallas kernels, body(): pl.pallas_call(finish_kernel, out_shape=jax.ShapeDtypeStruct(frames.shape...  1.82 us
    pallas_call x1, Pallas kernels, body(): pl.pallas_call(dispatch_kernel, out_shape=jax.ShapeDtypeStruct(exchange,...  1.55 us
    reduce_sum x1, other arithmetic, body(): jnp.sum(jnp.where(lane_session, context_len[:, None], 0), axis=0)[None, :]  1.4 us
  transfers between devices with their start and end apart: 1, of which 1 were waited for; matrix products, arithmetic and copies ran while one was open for 10% of the time, Pallas kernels for 0%

profile of v1, /device:TPU:1, one launch (start us, length us, event | category | flops | bytes accessed | tf_op | source)
XLA Modules:
  0.0 67.5 jit_solution(12878374650286267944)
XLA Ops:
  0.0 1.6 %dispatch.1 = bf16[16,16,2,256]{3,2,1,0:T(2,128)(2,1)} custom-call(s32[1]{0:T(128)} %bitcast.block_ref, s32[256]{0:T(256)} %session_ref.3, s32[256]{0:T(256)} %owner_ref.3, bf16[16,256]{1,0:T(8,128)(2,1)} %frames_ref.3), custom_call_target="tpu_custom_call" | custom-call | tf_op jit(solution)/shard_map/dispatch/pallas_call | solution.py:134
  1.6 15.7 %all-to-all-start = ((bf16[256,2,256]{2,1,0:T(2,128)(2,1)}), bf16[256,2,256]{2,1,0:T(2,128)(2,1)S(1)}, u32[]{:S(2)}, u32[]{:S(2)}) async-start(bf16[256,2,256]{2,1,0:T(2,128)(2,1)} %bitcast.11), calls=%async_computation | async-start | bytes 524288 | tf_op jit(solution)/shard_map/all_to_all | solution.py:142
  17.2 0.7 %broadcast_compare_fusion = pred[256]{0:T(512)(128)(4,1)S(1)} fusion(s32[256]{0:T(256)} %owner_ref.3, s32[]{:T(128)} %axis_index.15), kind=kLoop, calls=%fused_computation.23 | loop fusion | flops 256 | bytes 1284 | tf_op jit(solution)/shard_map/eq | solution.py:148
  17.9 0.9 %fusion.3 = pred[256]{0:T(512)(128)(4,1)S(1)} fusion(s32[256]{0:T(256)} %session_ref.3, pred[256]{0:T(512)(128)(4,1)S(1)} %broadcast_compare_fusion), kind=kLoop, calls=%fused_computation.8 | loop fusion | flops 196352 | bytes 1536 | tf_op jit(solution)/shard_map/reduce_or | solution.py:151
  18.8 0.1 convert_reduce_fusion
  18.9 0.9 %select_reduce_fusion = s32[256]{0:T(256)S(1)} fusion(s32[256]{0:T(256)S(1)} %convert_reduce_fusion, s32[256]{0:T(256)} %session_ref.3), kind=kLoop, calls=%fused_computation | loop fusion | flops 196352 | bytes 3072 | tf_op jit(solution)/shard_map/reduce_sum | solution.py:152
  19.8 0.2 convert_reduce_fusion.1
  20.0 0.1 select_reduce_fusion.2
  20.1 1.3 %reshape.88 = f32[4096]{0:T(1024)} convert(bf16[4096]{0:T(1024)(128)(2,1)} %param.9) | non-fusion elementwise | flops 4096 | bytes 24576 | tf_op jit(solution)/shard_map/reshape | solution.py:182
  21.4 1.4 %select_reduce_fusion.1 = s32[128]{0:T(128)} fusion(s32[256]{0:T(256)} %param.15, s32[128]{0:T(128)S(1)} %and_select_fusion, s32[256]{0:T(256)S(1)} %convert_reduce_fusion, pred[256]{0:T(512)(128)(4,1)S(1)} %broadcast_compare_fusion), kind=kLoop, calls=%fused_computation.10 | loop fusion | flops 130944 | bytes 3328 | tf_op jit(solution)/shard_map/reduce_sum | solution.py:165
  22.8 0.6 fusion.5.collect_ref
  23.4 0.7 compare_convert_fusion.place_ref
  24.1 8.8 %all-to-all-done = bf16[256,2,256]{2,1,0:T(2,128)(2,1)S(1)} async-done(((bf16[256,2,256]{2,1,0:T(2,128)(2,1)}), bf16[256,2,256]{2,1,0:T(2,128)(2,1)S(1)}, u32[]{:S(2)}, u32[]{:S(2)}) %all-to-all-start) | async-done | bytes 262176 | tf_op jit(solution)/shard_map/all_to_all | solution.py:142
  32.9 0.0 copy-start
  32.9 0.7 %copy-done = bf16[256,2,256]{2,1,0:T(2,128)(2,1)} copy-done((bf16[256,2,256]{2,1,0:T(2,128)(2,1)}, bf16[256,2,256]{2,1,0:T(2,128)(2,1)S(1)}, u32[]{:S(2)}) %copy-start) | copy-done | bytes 262168
  33.6 10.4 %attend.1 = bf16[16,16,2,256]{3,2,1,0:T(2,128)(2,1)} custom-call(bf16[16,16,2,256]{3,2,1,0:T(2,128)(2,1)} %bitcast.9, f32[1,4096]{1,0:T(1,128)} %bitcast.13, bf16[3,4096,128]{2,1,0:T(8,128)(2,1)} %w_ref.1, bf16[2,375,32,128]{3,2,1,0:T(8,128)(2,1)} %bitcast.8, bf16[128,4096]{1,0:T(8,128)(2,1)} %w_out_ref.1, bf16[32,32]{1,0:T(8,128)(2,1)} %fusion.5.collect_ref, ...), custom_call_target="tpu_custom_call" | custom-call | tf_op jit(solution)/shard_map/attend/pallas_call | solution.py:169
  44.0 21.7 %all_to_all.10 = bf16[256,2,256]{2,1,0:T(2,128)(2,1)} all-to-all(bf16[256,2,256]{2,1,0:T(2,128)(2,1)} %bitcast.10), channel_id=1, replica_groups=mesh['sess'=16,'tp'=16] {'sess','tp'}, dimensions={0} | all-to-all | bytes 524288 | tf_op jit(solution)/shard_map/all_to_all | solution.py:190
  65.7 1.8 %finish.1 = bf16[16,256]{1,0:T(8,128)(2,1)} custom-call(s32[1]{0:T(128)} %bitcast.block_ref, s32[256]{0:T(256)} %session_ref.3, s32[256]{0:T(256)} %owner_ref.3, bf16[16,16,2,256]{3,2,1,0:T(2,128)(2,1)} %bitcast.12, bf16[16,256]{1,0:T(8,128)(2,1)} %frames_ref.3), custom_call_target="tpu_custom_call" | custom-call | tf_op jit(solution)/shard_map/finish/pallas_call | solution.py:194
  (4 shorter events, 0.0 us)
Async XLA Ops:
  1.6 31.4 %all-to-all-start = ((bf16[256,2,256]{2,1,0:T(2,128)(2,1)}), bf16[256,2,256]{2,1,0:T(2,128)(2,1)S(1)}, u32[]{:S(2)}, u32[]{:S(2)}) async-start(bf16[256,2,256]{2,1,0:T(2,128)(2,1)} %bitcast.11), calls=%async_computation | async-start | bytes 524288 | tf_op jit(solution)/shard_map/all_to_all | solution.py:142
  32.9 0.7 %copy-start = (bf16[256,2,256]{2,1,0:T(2,128)(2,1)}, bf16[256,2,256]{2,1,0:T(2,128)(2,1)S(1)}, u32[]{:S(2)}) copy-start(bf16[256,2,256]{2,1,0:T(2,128)(2,1)S(1)} %all-to-all-done) | copy-start | bytes 786436

commit v2 on v1

--- a/solution.py
+++ b/solution.py
@@ -1,3 +1,5 @@
+import functools
+
 import jax
 import jax.numpy as jnp
 from jax import lax
@@ -10,6 +12,10 @@
 F32 = jnp.float32
 VM = pl.BlockSpec(memory_space=pltpu.VMEM)
 SM = pl.BlockSpec(memory_space=pltpu.SMEM)
+
+
+def near(*arrays):
+    return [pltpu.with_memory_space_constraint(a, pltpu.VMEM) for a in arrays]
 
 
 def row_targets(session_ref, owner_ref, block, rows, cap, count_ref, owners):
@@ -37,10 +43,64 @@
         out_ref[o] = jnp.broadcast_to(pair[None], (peers, cap, width))
 
 
+def table_kernel(
+    blocks, block_ref, session_ref, owner_ref, length_ref, gain_ref,
+    collect_ref, place_ref, lane_length_ref, wide_gain_ref,
+):
+    wide_gain_ref[...] = gain_ref[...].astype(F32)
+    sessions = session_ref.shape[1]
+    slots, places = collect_ref.shape
+    me = block_ref[0]
+
+    def iota(shape, dim):
+        return lax.broadcasted_iota(jnp.int32, shape, dim)
+
+    def dot(a, b, dims):
+        return lax.dot_general(
+            a.astype(BF), b.astype(BF), (dims, ((), ())), preferred_element_type=F32
+        )
+
+    def one(flag):
+        return jnp.where(flag, 1.0, 0.0)
+
+    square = (sessions, sessions)
+    before, after = iota(square, 0), iota(square, 1)
+    mine = jnp.broadcast_to(one(owner_ref[...] == me), (8, sessions))
+    slot_of = dot(mine, one(before < after), ((1,), (0,)))
+    rows_per_block = sessions // blocks
+    cap = places // blocks
+    matches = one(before == session_ref[...])
+    row_mine = dot(mine, matches, ((1,), (0,)))
+    row_slot = dot(slot_of, matches, ((1,), (0,)))[0:1].astype(jnp.int32)
+    same_block = (before // rows_per_block == after // rows_per_block) & (before < after)
+    row_pair = dot(row_mine, one(same_block), ((1,), (0,)))[0:1].astype(jnp.int32)
+    owned = row_mine[0:1] > 0.5
+    row_place = iota((1, sessions), 1) // rows_per_block * cap + row_pair
+    at_place = (iota((places, sessions), 0) == row_place) & owned
+    at_slot = (iota((slots, sessions), 0) == row_slot) & owned
+    collect_ref[...] = dot(one(at_slot), one(at_place), ((1,), (1,))).astype(BF)
+    place_slot = jnp.sum(jnp.where(at_place, row_slot + 1, 0), axis=1, keepdims=True) - 1
+    place_ref[...] = one(place_slot == iota((places, HD), 1) % slots)
+    lane_session = one(
+        (iota((HD, sessions), 0) % slots == slot_of[0:1].astype(jnp.int32)) & (mine[0:1] > 0.5)
+    )
+    length = jnp.broadcast_to(length_ref[...], (8, sessions))
+    high = dot((length >> 4).astype(F32), lane_session, ((1,), (1,)))
+    low = dot((length & 15).astype(F32), lane_session, ((1,), (1,)))
+    lane_length_ref[...] = (high * 16.0 + low)[0:1].astype(jnp.int32)
+
+
 def attend_kernel(
-    x_ref, gain_ref, w_ref, kv_ref, w_out_ref, collect_ref, place_ref, length_ref,
-    out_ref, rows_ref, score_ref, spread_ref,
+    x_ref, w_ref, collect_ref, place_ref, length_ref, gain_ref, kv_hbm, w_out_hbm,
+    out_ref, kv_ref, w_out_ref, sems, rows_ref, score_ref,
 ):
+    copies = [
+        pltpu.make_async_copy(kv_hbm.at[0], kv_ref.at[0], sems.at[0]),
+        pltpu.make_async_copy(kv_hbm.at[1], kv_ref.at[1], sems.at[1]),
+        pltpu.make_async_copy(w_out_hbm, w_out_ref, sems.at[2]),
+    ]
+    for copy in copies:
+        copy.start()
     owners, peers, cap, width = x_ref.shape
     places = owners * cap
     model = peers * width
@@ -52,7 +112,11 @@
             rows_ref[s * cap : (s + 1) * cap, t * width : (t + 1) * width] = x_ref[s, t]
     wide = rows_ref[...].astype(F32)
     scale = lax.rsqrt(jnp.sum(wide * wide, axis=1, keepdims=True) / model + 1e-05)
-    normed = (wide * scale * gain_ref[...]).astype(BF)
+    gains = gain_ref[...]
+    for k in range(model // HD):
+        part = rows_ref[:, k * HD : (k + 1) * HD].astype(F32)
+        rows_ref[:, k * HD : (k + 1) * HD] = (part * scale * gains[k : k + 1]).astype(BF)
+    normed = rows_ref[...]
     projected = [
         jnp.dot(normed, w_ref[c], preferred_element_type=F32).astype(BF) for c in range(3)
     ]
@@ -62,6 +126,7 @@
     ]
     lane = lax.broadcasted_iota(jnp.int32, (slots, HD), 1)
     own = lax.broadcasted_iota(jnp.int32, (slots, HD), 0) == lane % slots
+    copies[0].wait()
     for g in range(steps):
         if g < steps - 1:
             keys = kv_ref[0, g * group : (g + 1) * group].reshape(HD, HD)
@@ -90,6 +155,7 @@
         shift *= 2
     score_ref[0:steps, :] = expo / total
     place = place_ref[...] > 0.0
+    copies[1].wait()
     mixed = jnp.zeros((places, HD), F32)
     for g in range(steps):
         weights = jnp.where(place, score_ref[g : g + 1, :], 0.0).astype(BF)
@@ -100,6 +166,7 @@
             values = jnp.concatenate([tail, new_value], axis=0)
         mixed += jnp.dot(weights, values, preferred_element_type=F32)
     attended = mixed.astype(BF)
+    copies[2].wait()
     for t in range(peers):
         part = jnp.dot(
             attended, w_out_ref[:, t * width : (t + 1) * width], preferred_element_type=F32
@@ -122,13 +189,11 @@
 def body(frames, norm_gain, w_qkv, w_out, kv_cache, frame_session, owner_of, context_len):
     owners = lax.axis_size("sess")
     peers = lax.axis_size("tp")
-    me = lax.axis_index("sess")
     rows, width = frames.shape
     slots = kv_cache.shape[1]
-    sessions = frame_session.shape[0]
     cap = (slots + owners - 1) // owners
     places = owners * cap
-    block = me.reshape(1).astype(jnp.int32)
+    block = lax.axis_index("sess").reshape(1).astype(jnp.int32)
     exchange = (owners, peers, cap, width)
 
     outgoing = pl.pallas_call(
@@ -144,48 +209,41 @@
         ("sess", "tp"), split_axis=0, concat_axis=0, tiled=True,
     ).reshape(exchange)
 
-    session_ids = jnp.arange(sessions, dtype=jnp.int32)
-    mine = owner_of == me
-    slot_of = jnp.sum(mine[None, :] & (session_ids[None, :] < session_ids[:, None]), axis=1)
-    matches = frame_session[:, None] == session_ids[None, :]
-    row_mine = jnp.any(matches & mine[None, :], axis=1)
-    row_slot = jnp.sum(jnp.where(matches, slot_of[None, :], 0), axis=1)
-    row_block = session_ids // rows
-    earlier = (row_block[:, None] == row_block[None, :]) & (session_ids[None, :] < session_ids[:, None])
-    row_pair = jnp.sum(earlier & row_mine[None, :], axis=1)
-    row_place = jnp.where(row_mine, row_block * cap + row_pair, -1)
-    place_ids = jnp.arange(places, dtype=jnp.int32)
-    at_place = row_place[None, :] == place_ids[:, None]
-    place_slot = jnp.sum(jnp.where(at_place, row_slot[None, :] + 1, 0), axis=1) - 1
-    slot_ids = jnp.arange(slots, dtype=jnp.int32)
-    collect = (slot_ids[:, None] == place_slot[None, :]).astype(BF)
-    lane_slot = jnp.arange(HD, dtype=jnp.int32) % slots
-    place_mask = (place_slot[:, None] == lane_slot[None, :]).astype(F32)
-    lane_session = mine[:, None] & (slot_of[:, None] == lane_slot[None, :])
-    lengths = jnp.sum(jnp.where(lane_session, context_len[:, None], 0), axis=0)[None, :]
-
-    context = kv_cache.shape[2]
+    tables = pl.pallas_call(
+        functools.partial(table_kernel, owners),
+        out_shape=(
+            pltpu.VMEM((slots, places), BF),
+            pltpu.VMEM((places, HD), F32),
+            pltpu.VMEM((1, HD), jnp.int32),
+            pltpu.VMEM((norm_gain.size // HD, HD), F32),
+        ),
+        in_specs=[SM, VM, VM, VM, VM],
+        out_specs=(VM, VM, VM, VM),
+        compiler_params=pltpu.CompilerParams(vmem_limit_bytes=4 << 20),
+        cost_estimate=pl.CostEstimate(flops=10**9, bytes_accessed=10**6, transcendentals=0),
+        name="tables",
+    )(block, *[a.reshape(1, -1) for a in (frame_session, owner_of, context_len)], norm_gain.reshape(-1, HD))
+
+    cache = kv_cache.transpose(0, 2, 1, 3)
+    context = cache.shape[1]
     steps = (context + HD // slots) // (HD // slots)
     partial_rows = pl.pallas_call(
         attend_kernel,
-        out_shape=jax.ShapeDtypeStruct(exchange, BF),
-        in_specs=[VM] * 8,
+        out_shape=pltpu.VMEM(exchange, BF),
+        in_specs=[VM] * 6 + [pl.BlockSpec(memory_space=pltpu.HBM)] * 2,
         out_specs=VM,
         scratch_shapes=[
+            pltpu.VMEM(cache.shape, BF),
+            pltpu.VMEM(w_out.shape, BF),
+            pltpu.SemaphoreType.DMA((3,)),
             pltpu.VMEM((places, peers * width), BF),
             pltpu.VMEM((steps + (-steps) % 8, HD), F32),
-            pltpu.VMEM((8, HD), F32),
         ],
         name="attend",
+        compiler_params=pltpu.CompilerParams(vmem_limit_bytes=10 << 20),
     )(
-        arrived,
-        norm_gain.astype(F32).reshape(1, -1),
-        w_qkv,
-        kv_cache.transpose(0, 2, 1, 3),
-        w_out,
-        collect,
-        place_mask,
-        lengths,
+        *near(arrived, w_qkv, *tables),
+        *[pltpu.with_memory_space_constraint(a, pltpu.HBM) for a in (cache, w_out)],
     )
     parts = lax.all_to_all(
         partial_rows.reshape(owners * peers, cap, width),
@@ -202,7 +260,8 @@
             pltpu.SMEM((owners,), jnp.int32),
         ],
         name="finish",
-    )(block, frame_session, owner_of, parts, frames)
+        compiler_params=pltpu.CompilerParams(vmem_limit_bytes=4 << 20),
+    )(block, frame_session, owner_of, *near(parts, frames))
 
 
 def solution(mesh):

time: 67.9 us -> 62.7 us (0.923)
  other arithmetic: 6.82 us -> 0 us
  waiting for transfers between devices: 8.84 us -> 12.5 us
  Pallas kernels: 13.8 us -> 11.1 us
  local copies, waits for them, and re-layouts: 0.7 us -> 2.74 us
  blocking collectives: 21.7 us -> 20.4 us
    all_to_all x1, waiting for transfers between devices: 8.84 us -> 12.5 us  [body(): lax.all_to_all(outgoing.reshape(owners * peers, cap, width), ('sess', 'tp...]
    reduce_sum x5 -> x0, other arithmetic: 2.68 us -> none  [the longest x1 1.4 us: body(): jnp.sum(jnp.where(lane_session, context_len[:, None], 0), axis=0)[None, :]]
    pallas_call x1 -> x2, Pallas kernels: 10.4 us -> 7.95 us  [the longest x1 7.5 us: body(): pl.pallas_call(attend_kernel, out_shape=pltpu.VMEM(exchange, BF), in_spec...]
    unnamed x2 -> x16, local copies, waits for them, and re-layouts: 0.7 us -> 2.74 us
    reshape x1 -> x0, other arithmetic: 1.3 us -> none  [body(): norm_gain.astype(F32).reshape(1, -1)]
    convert_element_type x2 -> x0, other arithmetic: 1.28 us -> none  [the longest x1 0.67 us: body(): place_mask = (place_slot[:, None] == lane_slot[None, :]).astype(F32)]
    all_to_all x1, blocking collectives: 21.7 us -> 20.4 us  [body(): lax.all_to_all(partial_rows.reshape(owners * peers, cap, width), ('sess',...]
    reduce_or x1 -> x0, other arithmetic: 0.86 us -> none  [body(): row_mine = jnp.any(matches & mine[None, :], axis=1)]
  transfers between devices with their start and end apart: 1 -> 1, of which waited for: 1 -> 1; matrix products, arithmetic and copies ran while one was open for 10% -> 0% of each run, Pallas kernels for 0% -> 1%
where the time goes in v2:
time: 62.7 us; the launch traced here: 62.4 us
  blocking collectives  20.4 us (33%)
  starting transfers between devices  15.6 us (25%)
  waiting for transfers between devices  12.5 us (20%)
  Pallas kernels  11.1 us (18%)
  local copies, waits for them, and re-layouts  2.74 us (4%)
    all_to_all x1, blocking collectives, body(): lax.all_to_all(partial_rows.reshape(owners * peers, cap, width), ('sess',...  20.4 us
    all_to_all x1, starting transfers between devices, body(): lax.all_to_all(outgoing.reshape(owners * peers, cap, width), ('sess', 'tp...  15.6 us
    all_to_all x1, waiting for transfers between devices, body(): lax.all_to_all(outgoing.reshape(owners * peers, cap, width), ('sess', 'tp...  12.5 us
    pallas_call x1, Pallas kernels, body(): pl.pallas_call(attend_kernel, out_shape=pltpu.VMEM(exchange, BF), in_spec...  7.5 us
    unnamed x16, local copies, waits for them, and re-layouts  2.74 us
    pallas_call x1, Pallas kernels, body(): pl.pallas_call(dispatch_kernel, out_shape=jax.ShapeDtypeStruct(exchange,...  1.73 us
    pallas_call x1, Pallas kernels, body(): pl.pallas_call(finish_kernel, out_shape=jax.ShapeDtypeStruct(frames.shape...  1.42 us
  transfers between devices with their start and end apart: 1, of which 1 were waited for; matrix products, arithmetic and copies ran while one was open for 0% of the time, Pallas kernels for 1%

profile of v2, /device:TPU:1, one launch (start us, length us, event | category | flops | bytes accessed | tf_op | source)
XLA Modules:
  0.0 62.4 jit_solution(5927474350824562705)
XLA Ops:
  0.0 0.0 copy-start
  0.0 1.7 %dispatch.1 = bf16[16,16,2,256]{3,2,1,0:T(2,128)(2,1)} custom-call(s32[1]{0:T(128)} %bitcast.block_ref, s32[256]{0:T(256)} %session_ref.3, s32[256]{0:T(256)} %owner_ref.3, bf16[16,256]{1,0:T(8,128)(2,1)} %frames_ref.3), custom_call_target="tpu_custom_call" | custom-call | tf_op jit(solution)/shard_map/dispatch/pallas_call | solution.py:199
  1.7 15.6 %all-to-all-start = ((bf16[256,2,256]{2,1,0:T(2,128)(2,1)}), bf16[256,2,256]{2,1,0:T(2,128)(2,1)S(1)}, u32[]{:S(2)}, u32[]{:S(2)}) async-start(bf16[256,2,256]{2,1,0:T(2,128)(2,1)} %bitcast.18), calls=%async_computation | async-start | bytes 524288 | tf_op jit(solution)/shard_map/all_to_all | solution.py:207
  17.4 0.0 copy-start.2
  17.4 0.7 %copy-done.2 = s32[256]{0:T(256)S(1)} copy-done((s32[256]{0:T(256)S(1)}, s32[256]{0:T(256)}, u32[]{:S(2)}) %copy-start.2) | copy-done | bytes 1048
  18.1 0.0 copy-start.4
  18.1 0.7 %copy-done.4 = s32[256]{0:T(256)S(1)} copy-done((s32[256]{0:T(256)S(1)}, s32[256]{0:T(256)}, u32[]{:S(2)}) %copy-start.4) | copy-done | bytes 1048
  18.7 0.0 copy-start.6
  18.7 0.7 %copy-done.6 = bf16[4096]{0:T(1024)(128)(2,1)S(1)} copy-done((bf16[4096]{0:T(1024)(128)(2,1)S(1)}, bf16[4096]{0:T(1024)(128)(2,1)}, u32[]{:S(2)}) %copy-start.6) | copy-done | bytes 8216
  19.4 0.0 copy-start.7
  19.4 0.7 %copy-done.7 = s32[256]{0:T(256)S(1)} copy-done((s32[256]{0:T(256)S(1)}, s32[256]{0:T(256)}, u32[]{:S(2)}) %copy-start.7) | copy-done | bytes 1048
  20.1 0.5 tables.1
  20.6 0.0 copy-start.1
  20.6 0.0 copy-start.3
  20.6 0.0 copy-start.5
  20.6 12.5 %all-to-all-done = bf16[256,2,256]{2,1,0:T(2,128)(2,1)S(1)} async-done(((bf16[256,2,256]{2,1,0:T(2,128)(2,1)}), bf16[256,2,256]{2,1,0:T(2,128)(2,1)S(1)}, u32[]{:S(2)}, u32[]{:S(2)}) %all-to-all-start) | async-done | bytes 262176 | tf_op jit(solution)/shard_map/all_to_all | solution.py:207
  33.1 0.0 copy-done
  33.1 7.5 %attend.1 = bf16[16,16,2,256]{3,2,1,0:T(2,128)(2,1)S(1)} custom-call(bf16[16,16,2,256]{3,2,1,0:T(2,128)(2,1)S(1)} %bitcast.10, bf16[3,4096,128]{2,1,0:T(8,128)(2,1)S(1)} %copy-done, bf16[32,32]{1,0:T(8,128)(2,1)S(1)} %get-tuple-element.9.collect_ref, f32[32,128]{1,0:T(8,128)S(1)} %get-tuple-element.10.place_ref, s32[1,128]{1,0:T(1,128)S(1)} %get-tuple-element.11.length_ref, ...), custom_call_target="tpu_custom_call" | custom-call | tf_op jit(solution)/shard_map/attend/pallas_call | solution.py:230
  40.6 20.4 %all_to_all.10 = bf16[256,2,256]{2,1,0:T(2,128)(2,1)S(1)} all-to-all(bf16[256,2,256]{2,1,0:T(2,128)(2,1)S(1)} %bitcast.11), channel_id=1, replica_groups=mesh['sess'=16,'tp'=16] {'sess','tp'}, dimensions={0} | all-to-all | bytes 524288 | tf_op jit(solution)/shard_map/all_to_all | solution.py:248
  61.0 0.0 copy-done.1
  61.0 0.0 copy-done.3
  61.0 0.0 copy-done.5
  61.0 1.4 %finish.1 = bf16[16,256]{1,0:T(8,128)(2,1)} custom-call(s32[1]{0:T(128)} %bitcast.block_ref, s32[256]{0:T(256)S(1)} %copy-done.3, s32[256]{0:T(256)S(1)} %copy-done.5, bf16[16,16,2,256]{3,2,1,0:T(2,128)(2,1)S(1)} %bitcast.12, bf16[16,256]{1,0:T(8,128)(2,1)S(1)} %copy-done.1), custom_call_target="tpu_custom_call" | custom-call | tf_op jit(solution)/shard_map/finish/pallas_call | solution.py:252
Async XLA Ops:
  0.0 33.1 %copy-start = (bf16[3,4096,128]{2,1,0:T(8,128)(2,1)S(1)}, bf16[3,4096,128]{2,1,0:T(8,128)(2,1)}, u32[]{:S(2)}) copy-start(bf16[3,4096,128]{2,1,0:T(8,128)(2,1)} %w_ref.1) | copy-start | bytes 9437188
  1.7 31.4 %all-to-all-start = ((bf16[256,2,256]{2,1,0:T(2,128)(2,1)}), bf16[256,2,256]{2,1,0:T(2,128)(2,1)S(1)}, u32[]{:S(2)}, u32[]{:S(2)}) async-start(bf16[256,2,256]{2,1,0:T(2,128)(2,1)} %bitcast.18), calls=%async_computation | async-start | bytes 524288 | tf_op jit(solution)/shard_map/all_to_all | solution.py:207
  17.4 0.7 %copy-start.2 = (s32[256]{0:T(256)S(1)}, s32[256]{0:T(256)}, u32[]{:S(2)}) copy-start(s32[256]{0:T(256)} %session_ref.3) | copy-start | bytes 3076
  18.1 0.7 %copy-start.4 = (s32[256]{0:T(256)S(1)}, s32[256]{0:T(256)}, u32[]{:S(2)}) copy-start(s32[256]{0:T(256)} %owner_ref.3) | copy-start | bytes 3076
  18.7 0.7 %copy-start.6 = (bf16[4096]{0:T(1024)(128)(2,1)S(1)}, bf16[4096]{0:T(1024)(128)(2,1)}, u32[]{:S(2)}) copy-start(bf16[4096]{0:T(1024)(128)(2,1)} %param.9) | copy-start | bytes 24580
  19.4 0.7 %copy-start.7 = (s32[256]{0:T(256)S(1)}, s32[256]{0:T(256)}, u32[]{:S(2)}) copy-start(s32[256]{0:T(256)} %param.15) | copy-start | bytes 3076
  20.6 40.4 %copy-start.1 = (bf16[16,256]{1,0:T(8,128)(2,1)S(1)}, bf16[16,256]{1,0:T(8,128)(2,1)}, u32[]{:S(2)}) copy-start(bf16[16,256]{1,0:T(8,128)(2,1)} %frames_ref.3) | copy-start | bytes 24580
  20.6 40.4 %copy-start.3 = (s32[256]{0:T(256)S(1)}, s32[256]{0:T(256)}, u32[]{:S(2)}) copy-start(s32[256]{0:T(256)} %session_ref.3) | copy-start | bytes 3076
  20.6 40.4 %copy-start.5 = (s32[256]{0:T(256)S(1)}, s32[256]{0:T(256)}, u32[]{:S(2)}) copy-start(s32[256]{0:T(256)} %owner_ref.3) | copy-start | bytes 3076

commit v3 on v2

v3 whole, which is shorter than its diff:
```python
import functools

import jax
import jax.numpy as jnp
from jax import lax
from jax.experimental import pallas as pl
from jax.experimental.pallas import tpu as pltpu
from jax.sharding import PartitionSpec as P

HD = 128
BF = jnp.bfloat16
F32 = jnp.float32
I32 = jnp.int32
VM = pl.BlockSpec(memory_space=pltpu.VMEM)
HBM = pl.BlockSpec(memory_space=pltpu.HBM)


def near(*arrays):
    return [pltpu.with_memory_space_constraint(a, pltpu.VMEM) for a in arrays]


def far(*arrays):
    return [pltpu.with_memory_space_constraint(a, pltpu.HBM) for a in arrays]


def limit(mib):
    return pltpu.CompilerParams(vmem_limit_bytes=mib << 20)


def iota(shape, dim):
    return lax.broadcasted_iota(I32, shape, dim)


def dispatch_kernel(
    owners, cap, session_hbm, owner_hbm, frames_hbm, out_hbm,
    session_ref, owner_ref, frames_ref, held, out_ref, count_ref, in_sems, out_sem,
):
    copies = [
        pltpu.make_async_copy(session_hbm, session_ref, in_sems.at[0]),
        pltpu.make_async_copy(owner_hbm, owner_ref, in_sems.at[1]),
        pltpu.make_async_copy(frames_hbm, frames_ref, in_sems.at[2]),
    ]
    for copy in copies:
        copy.start()
    rows, width = frames_ref.shape
    pieces = width // HD
    chunk = cap * pieces
    held[...] = jnp.zeros_like(held)
    for o in range(owners):
        count_ref[o] = 0
    for copy in copies:
        copy.wait()
    first = lax.axis_index("sess") * rows
    wide = frames_ref[...].astype(F32)
    for r in range(rows):
        o = owner_ref[session_ref[first + r]]
        pair = count_ref[o]
        count_ref[o] = pair + 1
        for f in range(pieces):
            held[pl.ds(o * chunk + pair * pieces + f, 1), :] = wide[r : r + 1, f * HD : (f + 1) * HD]
    span = out_ref.shape[0] // owners
    for o in range(owners):
        piece = held[o * chunk : (o + 1) * chunk, :]
        tile = jnp.concatenate([piece] * (16 // chunk), axis=0).astype(BF)
        for k in range(span // 16):
            out_ref[o * span + k * 16 : o * span + (k + 1) * 16, :] = tile
    copy = pltpu.make_async_copy(out_ref, out_hbm, out_sem)
    copy.start()
    copy.wait()


def table_kernel(
    blocks, session_ref, owner_ref, length_ref, gain_ref,
    collect_ref, place_ref, lane_length_ref, wide_gain_ref, target_ref,
):
    wide_gain_ref[...] = gain_ref[...].astype(F32)
    sessions = session_ref.shape[1]
    slots, places = collect_ref.shape
    me = lax.axis_index("sess")

    def dot(a, b, dims):
        return lax.dot_general(
            a.astype(BF), b.astype(BF), (dims, ((), ())), preferred_element_type=F32
        )

    def one(flag):
        return jnp.where(flag, 1.0, 0.0)

    square = (sessions, sessions)
    before, after = iota(square, 0), iota(square, 1)
    owner_row = jnp.broadcast_to(owner_ref[...], (8, sessions))
    mine = one(owner_row == me)
    slot_of = dot(mine, one(before < after), ((1,), (0,)))
    rows = sessions // blocks
    matches = one(before == session_ref[...])
    row_mine = dot(mine, matches, ((1,), (0,)))
    row_slot = dot(slot_of, matches, ((1,), (0,)))[0:1].astype(I32)
    row_owner = dot(owner_row.astype(F32), matches, ((1,), (0,)))[0:1].astype(I32)
    same_block = (before // rows == after // rows) & (before < after)
    row_pair = dot(row_mine, one(same_block), ((1,), (0,)))[0:1].astype(I32)
    owned = row_mine[0:1] > 0.5
    row_place = row_pair * blocks + iota((1, sessions), 1) // rows
    at_place = (iota((places, sessions), 0) == row_place) & owned
    at_slot = (iota((slots, sessions), 0) == row_slot) & owned
    collect_ref[...] = dot(one(at_slot), one(at_place), ((1,), (1,))).astype(BF)
    place_slot = jnp.sum(jnp.where(at_place, row_slot + 1, 0), axis=1, keepdims=True) - 1
    place_ref[...] = one(place_slot == iota((places, HD), 1) % slots)
    lane_session = one(
        (iota((HD, sessions), 0) % slots == slot_of[0:1].astype(I32)) & (mine[0:1] > 0.5)
    )
    length = jnp.broadcast_to(length_ref[...], (8, sessions))
    high = dot((length >> 4).astype(F32), lane_session, ((1,), (1,)))
    low = dot((length & 15).astype(F32), lane_session, ((1,), (1,)))
    lane_length_ref[...] = (high * 16.0 + low)[0:1].astype(I32)
    local = (rows, sessions)
    row_id = iota(local, 1)
    own_id = me * rows + iota(local, 0)
    own_owner = jnp.sum(jnp.where(row_id == own_id, row_owner, 0), axis=1, keepdims=True)
    earlier = (row_id // rows == me) & (row_id < own_id) & (row_owner == own_owner)
    own_pair = jnp.sum(jnp.where(earlier, 1, 0), axis=1, keepdims=True)
    target_ref[...] = jnp.broadcast_to(own_pair * blocks + own_owner, target_ref.shape)


def turn(tiles):
    row = iota(tiles[0].shape, 0)
    for bit in (4, 2, 1):
        low = (row & bit) == 0
        turned = list(tiles)
        for v in range(8):
            if v & bit == 0:
                a, b = tiles[v], tiles[v + bit]
                turned[v] = jnp.where(low, a, pltpu.roll(b, bit, 0))
                turned[v + bit] = jnp.where(low, pltpu.roll(a, 8 - bit, 0), b)
        tiles = turned
    return tiles


def attend_kernel(
    owners, cap, pieces, x_ref, w_ref, collect_ref, place_ref, length_ref, gain_ref,
    kv_hbm, w_out_hbm, out_ref, kv_ref, w_out_ref, sems, exch_ref, rows_ref, score_ref,
):
    copies = [
        pltpu.make_async_copy(kv_hbm.at[0], kv_ref.at[0], sems.at[0]),
        pltpu.make_async_copy(kv_hbm.at[1], kv_ref.at[1], sems.at[1]),
        pltpu.make_async_copy(w_out_hbm, w_out_ref, sems.at[2]),
    ]
    for copy in copies:
        copy.start()
    places, model = rows_ref.shape
    span = x_ref.shape[0] // owners
    chunk = cap * pieces
    tiles = model // HD
    context, slots = kv_ref.shape[1], kv_ref.shape[2]
    group = HD // slots
    steps = (context + group) // group
    half = steps // 2

    block = 16 // chunk

    def unpack(i, carry):
        for h in range(owners // 8):
            parts = []
            for o in range(8):
                at = pl.multiple_of((h * 8 + o) * span + i * 16, 16)
                parts.append(x_ref[pl.ds(at, 16), :].astype(F32))
            for b in range(2):
                turned = turn([part[b * 8 : (b + 1) * 8] for part in parts])
                for v, tile in enumerate(turned):
                    row = b * 8 + v
                    t, j, f = row // chunk, row % chunk // pieces, row % pieces
                    k = (i * block + t) * pieces + f
                    exch_ref[k, j * owners + h * 8 : j * owners + h * 8 + 8, :] = tile
        return carry

    lax.fori_loop(0, span // 16, unpack, 0)

    squares = [jnp.zeros((places, HD), F32) for _ in range(2)]
    for k in range(tiles):
        part = exch_ref[k]
        squares[k % 2] += part * part
    scale = lax.rsqrt(jnp.sum(squares[0] + squares[1], axis=1, keepdims=True) / model + 1e-05)
    for k in range(tiles):
        cols = slice(k * HD, (k + 1) * HD)
        rows_ref[:, cols] = (exch_ref[k] * scale * gain_ref[k : k + 1, :]).astype(BF)

    deep = 2 * HD
    sums = [jnp.zeros((places, deep), F32) for _ in range(2)]
    for c in range(model // deep):
        at = slice(c * deep, (c + 1) * deep)
        both = jnp.concatenate([w_ref[0, at, :], w_ref[1, at, :]], axis=1)
        sums[c % 2] += jnp.dot(rows_ref[:, at], both, preferred_element_type=F32)
    query_key = (sums[0] + sums[1]).astype(BF)
    sums = [jnp.zeros((2 * places, deep), F32) for _ in range(2)]
    for c in range(model // deep // 2):
        low = slice(c * deep, (c + 1) * deep)
        high = slice(model // 2 + c * deep, model // 2 + (c + 1) * deep)
        both = jnp.concatenate([w_ref[2, low, :], w_ref[2, high, :]], axis=1)
        stacked = jnp.concatenate([rows_ref[:, low], rows_ref[:, high]], axis=0)
        sums[c % 2] += jnp.dot(stacked, both, preferred_element_type=F32)
    total = sums[0] + sums[1]
    value = (total[:places, :HD] + total[places:, HD:]).astype(BF)
    collect = collect_ref[...]
    query_key = jnp.dot(collect, query_key, preferred_element_type=F32).astype(BF)
    query, new_key = query_key[:, :HD], query_key[:, HD:]
    new_value = jnp.dot(collect, value, preferred_element_type=F32).astype(BF)

    own = iota((slots, HD), 0) == iota((slots, HD), 1) % slots
    copies[0].wait()
    for g in range(half):
        first = 2 * g * group
        last = min(first + 2 * group, context)
        keys = kv_ref[0, first:last].reshape((last - first) * slots, HD)
        if last - first < 2 * group:
            keys = jnp.concatenate([keys, new_key], axis=0)
        dots = lax.dot_general(
            query, keys, (((1,), (1,)), ((), ())), preferred_element_type=F32
        )
        for i in range(2):
            part = jnp.where(own, dots[:, i * HD : (i + 1) * HD], 0.0)
            score_ref[2 * g + i : 2 * g + i + 1, :] = jnp.sum(part, axis=0, keepdims=True)
    scores = score_ref[0:steps, :] * (1.0 / jnp.sqrt(F32(HD)))
    frame = iota((steps, HD), 0) * group + iota((steps, HD), 1) // slots
    valid = (frame < length_ref[...]) | (frame == context)
    scores = jnp.where(valid, scores, -jnp.inf)
    top = jnp.max(scores, axis=0, keepdims=True)
    shift = slots
    while shift < HD:
        top = jnp.maximum(top, pltpu.roll(top, shift, 1))
        shift *= 2
    expo = jnp.where(valid, jnp.exp(scores - top), 0.0)
    total = jnp.sum(expo, axis=0, keepdims=True)
    shift = slots
    while shift < HD:
        total = total + pltpu.roll(total, shift, 1)
        shift *= 2
    score_ref[0:steps, :] = expo / total

    place = place_ref[...] > 0.0

    def weights(step):
        return jnp.where(place, score_ref[step : step + 1, :], 0.0).astype(BF)

    def values(step, count):
        first = step * group
        last = min(first + count * group, context)
        found = kv_ref[1, first:last].reshape((last - first) * slots, HD)
        if last - first < count * group:
            found = jnp.concatenate([found, new_value], axis=0)
        return found

    copies[1].wait()
    sums = [jnp.zeros((2 * places, deep), F32) for _ in range(2)]
    for c in range((half + 1) // 2):
        count = min(2, half - 2 * c)
        left, right = 2 * c, half + 2 * c
        stacked = jnp.concatenate(
            [
                jnp.concatenate([weights(at + i) for i in range(count)], axis=1)
                for at in (left, right)
            ],
            axis=0,
        )
        both = jnp.concatenate([values(left, count), values(right, count)], axis=1)
        sums[c % 2] += jnp.dot(stacked, both, preferred_element_type=F32)
    total = sums[0] + sums[1]
    attended = (total[:places, :HD] + total[places:, HD:]).astype(BF)
    copies[2].wait()
    width = pieces * HD
    for i in range(span // 16):
        found = [
            jnp.dot(
                attended,
                w_out_ref[:, (i * block + t) * width : (i * block + t + 1) * width],
                preferred_element_type=F32,
            )
            for t in range(block)
        ]
        for h in range(owners // 8):
            turned = []
            for b in range(2):
                tiles_in = []
                for v in range(8):
                    row = b * 8 + v
                    t, j, f = row // chunk, row % chunk // pieces, row % pieces
                    first = j * owners + h * 8
                    tiles_in.append(found[t][first : first + 8, f * HD : (f + 1) * HD])
                turned.append(turn(tiles_in))
            for o in range(8):
                at = (h * 8 + o) * span + i * 16
                both = jnp.concatenate([turned[0][o], turned[1][o]], axis=0)
                out_ref[at : at + 16, :] = both.astype(BF)


def finish_kernel(owners, cap, parts_ref, frames_ref, target_ref, out_ref, sums_ref):
    rows, width = frames_ref.shape
    pieces = width // HD
    chunk = cap * pieces
    span = parts_ref.shape[0] // owners
    for o in range(owners):
        part = parts_ref[o * span : (o + 1) * span, :].astype(F32)
        part = jnp.sum(part.reshape(span // 8, 8, HD), axis=0)
        shift = chunk
        while shift < 8:
            part = part + pltpu.roll(part, shift, 0)
            shift *= 2
        sums_ref[o * chunk : (o + 1) * chunk, :] = part[:chunk]
    target = target_ref[...]
    found = [jnp.zeros((rows, HD), F32) for _ in range(pieces)]
    for o in range(owners):
        for j in range(cap):
            here = target == j * owners + o
            for f in range(pieces):
                at = o * chunk + j * pieces + f
                found[f] = jnp.where(here, sums_ref[at : at + 1, :], found[f])
    for f in range(pieces):
        cols = slice(f * HD, (f + 1) * HD)
        out_ref[:, cols] = (frames_ref[:, cols].astype(F32) + found[f]).astype(BF)


def exchanged(array):
    return lax.all_to_all(array, ("sess", "tp"), split_axis=0, concat_axis=0, tiled=True)


def body(frames, norm_gain, w_qkv, w_out, kv_cache, frame_session, owner_of, context_len):
    owners = lax.axis_size("sess")
    peers = lax.axis_size("tp")
    rows, width = frames.shape
    slots = kv_cache.shape[1]
    cap = (slots + owners - 1) // owners
    places = owners * cap
    pieces = width // HD
    exchange = (owners * peers * cap * pieces, HD)

    outgoing = pl.pallas_call(
        functools.partial(dispatch_kernel, owners, cap),
        out_shape=pltpu.HBM(exchange, BF),
        in_specs=[HBM, HBM, HBM],
        out_specs=HBM,
        scratch_shapes=[
            pltpu.SMEM(frame_session.shape, I32),
            pltpu.SMEM(owner_of.shape, I32),
            pltpu.VMEM(frames.shape, BF),
            pltpu.VMEM((places * pieces, HD), F32),
            pltpu.VMEM(exchange, BF),
            pltpu.SMEM((owners,), I32),
            pltpu.SemaphoreType.DMA((3,)),
            pltpu.SemaphoreType.DMA,
        ],
        compiler_params=limit(4),
        name="dispatch",
    )(*far(frame_session, owner_of, frames))
    arrived = exchanged(outgoing)

    tables = pl.pallas_call(
        functools.partial(table_kernel, owners),
        out_shape=(
            pltpu.VMEM((slots, places), BF),
            pltpu.VMEM((places, HD), F32),
            pltpu.VMEM((1, HD), I32),
            pltpu.VMEM((norm_gain.size // HD, HD), F32),
            pltpu.VMEM((rows, HD), I32),
        ),
        in_specs=[VM] * 4,
        out_specs=(VM,) * 5,
        compiler_params=limit(4),
        cost_estimate=pl.CostEstimate(flops=10**9, bytes_accessed=10**6, transcendentals=0),
        name="tables",
    )(
        *[a.reshape(1, -1) for a in (frame_session, owner_of, context_len)],
        norm_gain.reshape(-1, HD),
    )
    *tables, target = tables

    cache = kv_cache.transpose(0, 2, 1, 3)
    steps = (cache.shape[1] + HD // slots) // (HD // slots)
    partial_rows = pl.pallas_call(
        functools.partial(attend_kernel, owners, cap, pieces),
        out_shape=pltpu.VMEM(exchange, BF),
        in_specs=[VM] * 6 + [HBM, HBM],
        out_specs=VM,
        scratch_shapes=[
            pltpu.VMEM(cache.shape, BF),
            pltpu.VMEM(w_out.shape, BF),
            pltpu.SemaphoreType.DMA((3,)),
            pltpu.VMEM((peers * pieces, places, HD), F32),
            pltpu.VMEM((places, peers * width), BF),
            pltpu.VMEM((steps + (-steps) % 8, HD), F32),
        ],
        compiler_params=limit(10),
        name="attend",
    )(*near(arrived, w_qkv, *tables), *far(cache, w_out))
    parts = exchanged(partial_rows)
    return pl.pallas_call(
        functools.partial(finish_kernel, owners, cap),
        out_shape=jax.ShapeDtypeStruct(frames.shape, frames.dtype),
        in_specs=[VM] * 3,
        out_specs=VM,
        scratch_shapes=[pltpu.VMEM((places * pieces, HD), F32)],
        compiler_params=limit(4),
        name="finish",
    )(*near(parts, frames, target))


def solution(mesh):
    in_specs = (
        P("sess", "tp"),
        P(),
        P(None, None, "tp"),
        P("tp", None),
        P(None, "sess", None, "tp"),
        P(),
        P(),
        P(),
    )
    out_specs = P("sess", "tp")
    return jax.shard_map(body, mesh=mesh, in_specs=in_specs, out_specs=out_specs, check_vma=False)
```

time: 62.7 us -> 59.1 us (0.943)
  Pallas kernels: 11.1 us -> 7.49 us
    pallas_call x3, Pallas kernels: 10.6 us -> 7.03 us  [the longest x1 4.69 us: body(): pl.pallas_call(functools.partial(attend_kernel, owners, cap, pieces), out...]
    unnamed x16 -> x12, local copies, waits for them, and re-layouts: 2.74 us -> 2.73 us
where the time goes in v3:
time: 59.1 us; the launch traced here: 58.8 us
  blocking collectives  20.4 us (35%)
  starting transfers between devices  15.7 us (27%)
  waiting for transfers between devices  12.5 us (21%)
  Pallas kernels  7.49 us (13%)
  local copies, waits for them, and re-layouts  2.73 us (5%)
    all_to_all x1, blocking collectives, exchanged(): lax.all_to_all(array, ('sess', 'tp'), split_axis=0, concat_axis=0, tiled=...  20.4 us
    all_to_all x1, starting transfers between devices, exchanged(): lax.all_to_all(array, ('sess', 'tp'), split_axis=0, concat_axis=0, tiled=...  15.7 us
    all_to_all x1, waiting for transfers between devices, exchanged(): lax.all_to_all(array, ('sess', 'tp'), split_axis=0, concat_axis=0, tiled=...  12.5 us
    pallas_call x1, Pallas kernels, body(): pl.pallas_call(functools.partial(attend_kernel, owners, cap, pieces), out...  4.69 us
    unnamed x12, local copies, waits for them, and re-layouts  2.73 us
    pallas_call x1, Pallas kernels, body(): pl.pallas_call(functools.partial(dispatch_kernel, owners, cap), out_shape...  1.67 us
  transfers between devices with their start and end apart: 1, of which 1 were waited for; matrix products, arithmetic and copies ran while one was open for 0% of the time, Pallas kernels for 1%

profile of v3, /device:TPU:1, one launch (start us, length us, event | category | flops | bytes accessed | tf_op | source)
XLA Modules:
  0.0 58.8 jit_solution(653481668917733444)
XLA Ops:
  0.0 0.0 copy-start
  0.0 1.7 %dispatch.1 = bf16[1024,128]{1,0:T(8,128)(2,1)} custom-call(s32[256]{0:T(256)} %session_hbm.1, s32[256]{0:T(256)} %owner_hbm.1, bf16[16,256]{1,0:T(8,128)(2,1)} %frames_ref.1), custom_call_target="tpu_custom_call" | custom-call | tf_op jit(solution)/shard_map/dispatch/pallas_call | solution.py:334
  1.7 15.7 %all-to-all-start = ((bf16[256,4,128]{2,1,0:T(4,128)(2,1)}), bf16[256,4,128]{2,1,0:T(4,128)(2,1)S(1)}, u32[]{:S(2)}, u32[]{:S(2)}) async-start(bf16[256,4,128]{2,1,0:T(4,128)(2,1)} %bitcast.17), calls=%async_computation | async-start | bytes 524288 | tf_op jit(solution)/shard_map/all_to_all | solution.py:321
  17.3 0.0 copy-start.2
  17.4 0.7 %copy-done.2 = s32[256]{0:T(256)S(1)} copy-done((s32[256]{0:T(256)S(1)}, s32[256]{0:T(256)}, u32[]{:S(2)}) %copy-start.2) | copy-done | bytes 1048
  18.0 0.0 copy-start.3
  18.0 0.7 %copy-done.3 = s32[256]{0:T(256)S(1)} copy-done((s32[256]{0:T(256)S(1)}, s32[256]{0:T(256)}, u32[]{:S(2)}) %copy-start.3) | copy-done | bytes 1048
  18.7 0.0 copy-start.4
  18.7 0.7 %copy-done.4 = bf16[4096]{0:T(1024)(128)(2,1)S(1)} copy-done((bf16[4096]{0:T(1024)(128)(2,1)S(1)}, bf16[4096]{0:T(1024)(128)(2,1)}, u32[]{:S(2)}) %copy-start.4) | copy-done | bytes 8216
  19.4 0.0 copy-start.5
  19.4 0.7 %copy-done.5 = s32[256]{0:T(256)S(1)} copy-done((s32[256]{0:T(256)S(1)}, s32[256]{0:T(256)}, u32[]{:S(2)}) %copy-start.5) | copy-done | bytes 1048
  20.1 0.5 tables.1
  20.5 0.0 copy-start.1
  20.5 12.5 %all-to-all-done = bf16[256,4,128]{2,1,0:T(4,128)(2,1)S(1)} async-done(((bf16[256,4,128]{2,1,0:T(4,128)(2,1)}), bf16[256,4,128]{2,1,0:T(4,128)(2,1)S(1)}, u32[]{:S(2)}, u32[]{:S(2)}) %all-to-all-start) | async-done | bytes 262176 | tf_op jit(solution)/shard_map/all_to_all | solution.py:321
  33.0 0.0 copy-done
  33.0 4.7 %attend.1 = bf16[1024,128]{1,0:T(8,128)(2,1)S(1)} custom-call(bf16[1024,128]{1,0:T(8,128)(2,1)S(1)} %bitcast.9, bf16[3,4096,128]{2,1,0:T(8,128)(2,1)S(1)} %copy-done, bf16[32,32]{1,0:T(8,128)(2,1)S(1)} %get-tuple-element.10.collect_ref, f32[32,128]{1,0:T(8,128)S(1)} %get-tuple-element.11.place_ref, s32[1,128]{1,0:T(1,128)S(1)} %get-tuple-element.12.length_ref, ...), custom_call_target="tpu_custom_call" | custom-call | tf_op jit(solution)/shard_map/attend/pallas_call | solution.py:376
  37.7 20.4 %all_to_all.22 = bf16[256,4,128]{2,1,0:T(4,128)(2,1)S(1)} all-to-all(bf16[256,4,128]{2,1,0:T(4,128)(2,1)S(1)} %bitcast.10), channel_id=1, replica_groups=mesh['sess'=16,'tp'=16] {'sess','tp'}, dimensions={0} | all-to-all | bytes 524288 | tf_op jit(solution)/shard_map/all_to_all | solution.py:321
  58.1 0.0 copy-done.1
  58.1 0.7 %finish.1 = bf16[16,256]{1,0:T(8,128)(2,1)} custom-call(bf16[1024,128]{1,0:T(8,128)(2,1)S(1)} %bitcast.11, bf16[16,256]{1,0:T(8,128)(2,1)S(1)} %copy-done.1, s32[16,128]{1,0:T(8,128)S(1)} %get-tuple-element.14.target_ref), custom_call_target="tpu_custom_call" | custom-call | tf_op jit(solution)/shard_map/finish/pallas_call | solution.py:393
Async XLA Ops:
  0.0 33.0 %copy-start = (bf16[3,4096,128]{2,1,0:T(8,128)(2,1)S(1)}, bf16[3,4096,128]{2,1,0:T(8,128)(2,1)}, u32[]{:S(2)}) copy-start(bf16[3,4096,128]{2,1,0:T(8,128)(2,1)} %w_ref.1) | copy-start | bytes 9437188
  1.7 31.4 %all-to-all-start = ((bf16[256,4,128]{2,1,0:T(4,128)(2,1)}), bf16[256,4,128]{2,1,0:T(4,128)(2,1)S(1)}, u32[]{:S(2)}, u32[]{:S(2)}) async-start(bf16[256,4,128]{2,1,0:T(4,128)(2,1)} %bitcast.17), calls=%async_computation | async-start | bytes 524288 | tf_op jit(solution)/shard_map/all_to_all | solution.py:321
  17.3 0.7 %copy-start.2 = (s32[256]{0:T(256)S(1)}, s32[256]{0:T(256)}, u32[]{:S(2)}) copy-start(s32[256]{0:T(256)} %session_hbm.1) | copy-start | bytes 3076
  18.0 0.7 %copy-start.3 = (s32[256]{0:T(256)S(1)}, s32[256]{0:T(256)}, u32[]{:S(2)}) copy-start(s32[256]{0:T(256)} %owner_hbm.1) | copy-start | bytes 3076
  18.7 0.7 %copy-start.4 = (bf16[4096]{0:T(1024)(128)(2,1)S(1)}, bf16[4096]{0:T(1024)(128)(2,1)}, u32[]{:S(2)}) copy-start(bf16[4096]{0:T(1024)(128)(2,1)} %param.9) | copy-start | bytes 24580
  19.4 0.7 %copy-start.5 = (s32[256]{0:T(256)S(1)}, s32[256]{0:T(256)}, u32[]{:S(2)}) copy-start(s32[256]{0:T(256)} %param.15) | copy-start | bytes 3076
  20.5 37.6 %copy-start.1 = (bf16[16,256]{1,0:T(8,128)(2,1)S(1)}, bf16[16,256]{1,0:T(8,128)(2,1)}, u32[]{:S(2)}) copy-start(bf16[16,256]{1,0:T(8,128)(2,1)} %frames_ref.1) | copy-start | bytes 24580

commit v4 on v3

--- a/solution.py
+++ b/solution.py
@@ -137,7 +137,7 @@
 
 def attend_kernel(
     owners, cap, pieces, x_ref, w_ref, collect_ref, place_ref, length_ref, gain_ref,
-    kv_hbm, w_out_hbm, out_ref, kv_ref, w_out_ref, sems, exch_ref, rows_ref, score_ref,
+    kv_hbm, w_out_hbm, out_ref, kv_ref, w_out_ref, sems, exch_ref, rows_ref, score_ref, sum_ref,
 ):
     copies = [
         pltpu.make_async_copy(kv_hbm.at[0], kv_ref.at[0], sems.at[0]),
@@ -189,7 +189,8 @@
         at = slice(c * deep, (c + 1) * deep)
         both = jnp.concatenate([w_ref[0, at, :], w_ref[1, at, :]], axis=1)
         sums[c % 2] += jnp.dot(rows_ref[:, at], both, preferred_element_type=F32)
-    query_key = (sums[0] + sums[1]).astype(BF)
+    for i in range(2):
+        sum_ref[i, :places] = sums[i]
     sums = [jnp.zeros((2 * places, deep), F32) for _ in range(2)]
     for c in range(model // deep // 2):
         low = slice(c * deep, (c + 1) * deep)
@@ -197,98 +198,110 @@
         both = jnp.concatenate([w_ref[2, low, :], w_ref[2, high, :]], axis=1)
         stacked = jnp.concatenate([rows_ref[:, low], rows_ref[:, high]], axis=0)
         sums[c % 2] += jnp.dot(stacked, both, preferred_element_type=F32)
-    total = sums[0] + sums[1]
-    value = (total[:places, :HD] + total[places:, HD:]).astype(BF)
-    collect = collect_ref[...]
-    query_key = jnp.dot(collect, query_key, preferred_element_type=F32).astype(BF)
-    query, new_key = query_key[:, :HD], query_key[:, HD:]
-    new_value = jnp.dot(collect, value, preferred_element_type=F32).astype(BF)
-
-    own = iota((slots, HD), 0) == iota((slots, HD), 1) % slots
-    copies[0].wait()
-    for g in range(half):
-        first = 2 * g * group
-        last = min(first + 2 * group, context)
-        keys = kv_ref[0, first:last].reshape((last - first) * slots, HD)
-        if last - first < 2 * group:
-            keys = jnp.concatenate([keys, new_key], axis=0)
-        dots = lax.dot_general(
-            query, keys, (((1,), (1,)), ((), ())), preferred_element_type=F32
-        )
+    for i in range(2):
+        sum_ref[2 + i] = sums[i]
+    live = lax.axis_index("sess") >= 0
+
+    @pl.when(live)
+    def _():
+        query_key = (sum_ref[0, :places] + sum_ref[1, :places]).astype(BF)
+        total = sum_ref[2] + sum_ref[3]
+        value = (total[:places, :HD] + total[places:, HD:]).astype(BF)
+        collect = collect_ref[...]
+        query_key = jnp.dot(collect, query_key, preferred_element_type=F32).astype(BF)
+        query, new_key = query_key[:, :HD], query_key[:, HD:]
+        new_value = jnp.dot(collect, value, preferred_element_type=F32).astype(BF)
+
+        own = iota((slots, HD), 0) == iota((slots, HD), 1) % slots
+        copies[0].wait()
+        for g in range(half):
+            first = 2 * g * group
+            last = min(first + 2 * group, context)
+            keys = kv_ref[0, first:last].reshape((last - first) * slots, HD)
+            if last - first < 2 * group:
+                keys = jnp.concatenate([keys, new_key], axis=0)
+            dots = lax.dot_general(
+                query, keys, (((1,), (1,)), ((), ())), preferred_element_type=F32
+            )
+            for i in range(2):
+                part = jnp.where(own, dots[:, i * HD : (i + 1) * HD], 0.0)
+                score_ref[2 * g + i : 2 * g + i + 1, :] = jnp.sum(part, axis=0, keepdims=True)
+        scores = score_ref[0:steps, :] * (1.0 / jnp.sqrt(F32(HD)))
+        frame = iota((steps, HD), 0) * group + iota((steps, HD), 1) // slots
+        valid = (frame < length_ref[...]) | (frame == context)
+        scores = jnp.where(valid, scores, -jnp.inf)
+        top = jnp.max(scores, axis=0, keepdims=True)
+        shift = slots
+        while shift < HD:
+            top = jnp.maximum(top, pltpu.roll(top, shift, 1))
+            shift *= 2
+        expo = jnp.where(valid, jnp.exp(scores - top), 0.0)
+        total = jnp.sum(expo, axis=0, keepdims=True)
+        shift = slots
+        while shift < HD:
+            total = total + pltpu.roll(total, shift, 1)
+            shift *= 2
+        score_ref[0:steps, :] = expo / total
+
+        place = place_ref[...] > 0.0
+
+        def weights(step):
+            return jnp.where(place, score_ref[step : step + 1, :], 0.0).astype(BF)
+
+        def values(step, count):
+            first = step * group
+            last = min(first + count * group, context)
+            found = kv_ref[1, first:last].reshape((last - first) * slots, HD)
+            if last - first < count * group:
+                found = jnp.concatenate([found, new_value], axis=0)
+            return found
+
+        copies[1].wait()
+        sums = [jnp.zeros((2 * places, deep), F32) for _ in range(2)]
+        for c in range((half + 1) // 2):
+            count = min(2, half - 2 * c)
+            left, right = 2 * c, half + 2 * c
+            stacked = jnp.concatenate(
+                [
+                    jnp.concatenate([weights(at + i) for i in range(count)], axis=1)
+                    for at in (left, right)
+                ],
+                axis=0,
+            )
+            both = jnp.concatenate([values(left, count), values(right, count)], axis=1)
+            sums[c % 2] += jnp.dot(stacked, both, preferred_element_type=F32)
         for i in range(2):
-            part = jnp.where(own, dots[:, i * HD : (i + 1) * HD], 0.0)
-            score_ref[2 * g + i : 2 * g + i + 1, :] = jnp.sum(part, axis=0, keepdims=True)
-    scores = score_ref[0:steps, :] * (1.0 / jnp.sqrt(F32(HD)))
-    frame = iota((steps, HD), 0) * group + iota((steps, HD), 1) // slots
-    valid = (frame < length_ref[...]) | (frame == context)
-    scores = jnp.where(valid, scores, -jnp.inf)
-    top = jnp.max(scores, axis=0, keepdims=True)
-    shift = slots
-    while shift < HD:
-        top = jnp.maximum(top, pltpu.roll(top, shift, 1))
-        shift *= 2
-    expo = jnp.where(valid, jnp.exp(scores - top), 0.0)
-    total = jnp.sum(expo, axis=0, keepdims=True)
-    shift = slots
-    while shift < HD:
-        total = total + pltpu.roll(total, shift, 1)
-        shift *= 2
-    score_ref[0:steps, :] = expo / total
-
-    place = place_ref[...] > 0.0
-
-    def weights(step):
-        return jnp.where(place, score_ref[step : step + 1, :], 0.0).astype(BF)
-
-    def values(step, count):
-        first = step * group
-        last = min(first + count * group, context)
-        found = kv_ref[1, first:last].reshape((last - first) * slots, HD)
-        if last - first < count * group:
-            found = jnp.concatenate([found, new_value], axis=0)
-        return found
-
-    copies[1].wait()
-    sums = [jnp.zeros((2 * places, deep), F32) for _ in range(2)]
-    for c in range((half + 1) // 2):
-        count = min(2, half - 2 * c)
-        left, right = 2 * c, half + 2 * c
-        stacked = jnp.concatenate(
-            [
-                jnp.concatenate([weights(at + i) for i in range(count)], axis=1)
-                for at in (left, right)
-            ],
-            axis=0,
-        )
-        both = jnp.concatenate([values(left, count), values(right, count)], axis=1)
-        sums[c % 2] += jnp.dot(stacked, both, preferred_element_type=F32)
-    total = sums[0] + sums[1]
-    attended = (total[:places, :HD] + total[places:, HD:]).astype(BF)
-    copies[2].wait()
-    width = pieces * HD
-    for i in range(span // 16):
-        found = [
-            jnp.dot(
-                attended,
-                w_out_ref[:, (i * block + t) * width : (i * block + t + 1) * width],
-                preferred_element_type=F32,
-            )
-            for t in range(block)
-        ]
-        for h in range(owners // 8):
-            turned = []
-            for b in range(2):
-                tiles_in = []
-                for v in range(8):
-                    row = b * 8 + v
-                    t, j, f = row // chunk, row % chunk // pieces, row % pieces
-                    first = j * owners + h * 8
-                    tiles_in.append(found[t][first : first + 8, f * HD : (f + 1) * HD])
-                turned.append(turn(tiles_in))
-            for o in range(8):
-                at = (h * 8 + o) * span + i * 16
-                both = jnp.concatenate([turned[0][o], turned[1][o]], axis=0)
-                out_ref[at : at + 16, :] = both.astype(BF)
+            sum_ref[i] = sums[i]
+
+        @pl.when(live)
+        def _():
+            total = sum_ref[0] + sum_ref[1]
+            attended = (total[:places, :HD] + total[places:, HD:]).astype(BF)
+            copies[2].wait()
+            width = pieces * HD
+            for i in range(span // 16):
+                found = [
+                    jnp.dot(
+                        attended,
+                        w_out_ref[:, (i * block + t) * width : (i * block + t + 1) * width],
+                        preferred_element_type=F32,
+                    )
+                    for t in range(block)
+                ]
+                for h in range(owners // 8):
+                    turned = []
+                    for b in range(2):
+                        tiles_in = []
+                        for v in range(8):
+                            row = b * 8 + v
+                            t, j, f = row // chunk, row % chunk // pieces, row % pieces
+                            first = j * owners + h * 8
+                            tiles_in.append(found[t][first : first + 8, f * HD : (f + 1) * HD])
+                        turned.append(turn(tiles_in))
+                    for o in range(8):
+                        at = (h * 8 + o) * span + i * 16
+                        both = jnp.concatenate([turned[0][o], turned[1][o]], axis=0)
+                        out_ref[at : at + 16, :] = both.astype(BF)
 
 
 def finish_kernel(owners, cap, parts_ref, frames_ref, target_ref, out_ref, sums_ref):
@@ -385,6 +398,7 @@
             pltpu.VMEM((peers * pieces, places, HD), F32),
             pltpu.VMEM((places, peers * width), BF),
             pltpu.VMEM((steps + (-steps) % 8, HD), F32),
+            pltpu.VMEM((4, 2 * places, 2 * HD), F32),
         ],
         compiler_params=limit(10),
         name="attend",

time: 59.1 us -> 58.8 us (level)
  no operation moved by 1% of the time
where the time goes in v4:
time: 58.8 us; the launch traced here: 58.5 us
  blocking collectives  20.4 us (35%)
  starting transfers between devices  15.7 us (27%)
  waiting for transfers between devices  12.5 us (21%)
  Pallas kernels  7.17 us (12%)
  local copies, waits for them, and re-layouts  2.73 us (5%)
    all_to_all x1, blocking collectives, exchanged(): lax.all_to_all(array, ('sess', 'tp'), split_axis=0, concat_axis=0, tiled=...  20.4 us
    all_to_all x1, starting transfers between devices, exchanged(): lax.all_to_all(array, ('sess', 'tp'), split_axis=0, concat_axis=0, tiled=...  15.7 us
    all_to_all x1, waiting for transfers between devices, exchanged(): lax.all_to_all(array, ('sess', 'tp'), split_axis=0, concat_axis=0, tiled=...  12.5 us
    pallas_call x1, Pallas kernels, body(): pl.pallas_call(functools.partial(attend_kernel, owners, cap, pieces), out...  4.37 us
    unnamed x12, local copies, waits for them, and re-layouts  2.73 us
    pallas_call x1, Pallas kernels, body(): pl.pallas_call(functools.partial(dispatch_kernel, owners, cap), out_shape...  1.67 us
  transfers between devices with their start and end apart: 1, of which 1 were waited for; matrix products, arithmetic and copies ran while one was open for 0% of the time, Pallas kernels for 1%

profile of v4, /device:TPU:1, one launch (start us, length us, event | category | flops | bytes accessed | tf_op | source)
XLA Modules:
  0.0 58.5 jit_solution(12691550875262090065)
XLA Ops:
  0.0 0.0 copy-start
  0.0 1.7 %dispatch.1 = bf16[1024,128]{1,0:T(8,128)(2,1)} custom-call(s32[256]{0:T(256)} %session_hbm.1, s32[256]{0:T(256)} %owner_hbm.1, bf16[16,256]{1,0:T(8,128)(2,1)} %frames_ref.1), custom_call_target="tpu_custom_call" | custom-call | tf_op jit(solution)/shard_map/dispatch/pallas_call | solution.py:347
  1.7 15.7 %all-to-all-start = ((bf16[256,4,128]{2,1,0:T(4,128)(2,1)}), bf16[256,4,128]{2,1,0:T(4,128)(2,1)S(1)}, u32[]{:S(2)}, u32[]{:S(2)}) async-start(bf16[256,4,128]{2,1,0:T(4,128)(2,1)} %bitcast.17), calls=%async_computation | async-start | bytes 524288 | tf_op jit(solution)/shard_map/all_to_all | solution.py:334
  17.3 0.0 copy-start.2
  17.4 0.7 %copy-done.2 = s32[256]{0:T(256)S(1)} copy-done((s32[256]{0:T(256)S(1)}, s32[256]{0:T(256)}, u32[]{:S(2)}) %copy-start.2) | copy-done | bytes 1048
  18.0 0.0 copy-start.3
  18.0 0.7 %copy-done.3 = s32[256]{0:T(256)S(1)} copy-done((s32[256]{0:T(256)S(1)}, s32[256]{0:T(256)}, u32[]{:S(2)}) %copy-start.3) | copy-done | bytes 1048
  18.7 0.0 copy-start.4
  18.7 0.7 %copy-done.4 = bf16[4096]{0:T(1024)(128)(2,1)S(1)} copy-done((bf16[4096]{0:T(1024)(128)(2,1)S(1)}, bf16[4096]{0:T(1024)(128)(2,1)}, u32[]{:S(2)}) %copy-start.4) | copy-done | bytes 8216
  19.4 0.0 copy-start.5
  19.4 0.7 %copy-done.5 = s32[256]{0:T(256)S(1)} copy-done((s32[256]{0:T(256)S(1)}, s32[256]{0:T(256)}, u32[]{:S(2)}) %copy-start.5) | copy-done | bytes 1048
  20.1 0.5 tables.1
  20.5 0.0 copy-start.1
  20.5 12.5 %all-to-all-done = bf16[256,4,128]{2,1,0:T(4,128)(2,1)S(1)} async-done(((bf16[256,4,128]{2,1,0:T(4,128)(2,1)}), bf16[256,4,128]{2,1,0:T(4,128)(2,1)S(1)}, u32[]{:S(2)}, u32[]{:S(2)}) %all-to-all-start) | async-done | bytes 262176 | tf_op jit(solution)/shard_map/all_to_all | solution.py:334
  33.0 0.0 copy-done
  33.0 4.4 %attend.1 = bf16[1024,128]{1,0:T(8,128)(2,1)S(1)} custom-call(bf16[1024,128]{1,0:T(8,128)(2,1)S(1)} %bitcast.9, bf16[3,4096,128]{2,1,0:T(8,128)(2,1)S(1)} %copy-done, bf16[32,32]{1,0:T(8,128)(2,1)S(1)} %get-tuple-element.10.collect_ref, f32[32,128]{1,0:T(8,128)S(1)} %get-tuple-element.11.place_ref, s32[1,128]{1,0:T(1,128)S(1)} %get-tuple-element.12.length_ref, ...), custom_call_target="tpu_custom_call" | custom-call | tf_op jit(solution)/shard_map/attend/pallas_call | solution.py:389
  37.4 20.4 %all_to_all.22 = bf16[256,4,128]{2,1,0:T(4,128)(2,1)S(1)} all-to-all(bf16[256,4,128]{2,1,0:T(4,128)(2,1)S(1)} %bitcast.10), channel_id=1, replica_groups=mesh['sess'=16,'tp'=16] {'sess','tp'}, dimensions={0} | all-to-all | bytes 524288 | tf_op jit(solution)/shard_map/all_to_all | solution.py:334
  57.8 0.0 copy-done.1
  57.8 0.7 %finish.1 = bf16[16,256]{1,0:T(8,128)(2,1)} custom-call(bf16[1024,128]{1,0:T(8,128)(2,1)S(1)} %bitcast.11, bf16[16,256]{1,0:T(8,128)(2,1)S(1)} %copy-done.1, s32[16,128]{1,0:T(8,128)S(1)} %get-tuple-element.14.target_ref), custom_call_target="tpu_custom_call" | custom-call | tf_op jit(solution)/shard_map/finish/pallas_call | solution.py:407
Async XLA Ops:
  0.0 33.0 %copy-start = (bf16[3,4096,128]{2,1,0:T(8,128)(2,1)S(1)}, bf16[3,4096,128]{2,1,0:T(8,128)(2,1)}, u32[]{:S(2)}) copy-start(bf16[3,4096,128]{2,1,0:T(8,128)(2,1)} %w_ref.1) | copy-start | bytes 9437188
  1.7 31.4 %all-to-all-start = ((bf16[256,4,128]{2,1,0:T(4,128)(2,1)}), bf16[256,4,128]{2,1,0:T(4,128)(2,1)S(1)}, u32[]{:S(2)}, u32[]{:S(2)}) async-start(bf16[256,4,128]{2,1,0:T(4,128)(2,1)} %bitcast.17), calls=%async_computation | async-start | bytes 524288 | tf_op jit(solution)/shard_map/all_to_all | solution.py:334
  17.3 0.7 %copy-start.2 = (s32[256]{0:T(256)S(1)}, s32[256]{0:T(256)}, u32[]{:S(2)}) copy-start(s32[256]{0:T(256)} %session_hbm.1) | copy-start | bytes 3076
  18.0 0.7 %copy-start.3 = (s32[256]{0:T(256)S(1)}, s32[256]{0:T(256)}, u32[]{:S(2)}) copy-start(s32[256]{0:T(256)} %owner_hbm.1) | copy-start | bytes 3076
  18.7 0.7 %copy-start.4 = (bf16[4096]{0:T(1024)(128)(2,1)S(1)}, bf16[4096]{0:T(1024)(128)(2,1)}, u32[]{:S(2)}) copy-start(bf16[4096]{0:T(1024)(128)(2,1)} %param.9) | copy-start | bytes 24580
  19.4 0.7 %copy-start.5 = (s32[256]{0:T(256)S(1)}, s32[256]{0:T(256)}, u32[]{:S(2)}) copy-start(s32[256]{0:T(256)} %param.15) | copy-start | bytes 3076
  20.5 37.3 %copy-start.1 = (bf16[16,256]{1,0:T(8,128)(2,1)S(1)}, bf16[16,256]{1,0:T(8,128)(2,1)}, u32[]{:S(2)}) copy-start(bf16[16,256]{1,0:T(8,128)(2,1)} %frames_ref.1) | copy-start | bytes 24580

commit v5 on v4

--- a/solution.py
+++ b/solution.py
@@ -8,6 +8,7 @@
 from jax.sharding import PartitionSpec as P
 
 HD = 128
+KEY_BLOCK = 192
 BF = jnp.bfloat16
 F32 = jnp.float32
 I32 = jnp.int32
@@ -31,52 +32,26 @@
     return lax.broadcasted_iota(I32, shape, dim)
 
 
-def dispatch_kernel(
-    owners, cap, session_hbm, owner_hbm, frames_hbm, out_hbm,
-    session_ref, owner_ref, frames_ref, held, out_ref, count_ref, in_sems, out_sem,
+def table_kernel(
+    chips, cores, cap, session_hbm, owner_hbm, length_hbm, gain_hbm, frames_hbm,
+    collect_ref, place_ref, lane_length_ref, wide_gain_ref, target_ref, send_ref, frames_ref,
+    session_ref, owner_ref, length_ref, gain_ref, sems,
 ):
-    copies = [
-        pltpu.make_async_copy(session_hbm, session_ref, in_sems.at[0]),
-        pltpu.make_async_copy(owner_hbm, owner_ref, in_sems.at[1]),
-        pltpu.make_async_copy(frames_hbm, frames_ref, in_sems.at[2]),
-    ]
+    pairs = (
+        (session_hbm, session_ref), (owner_hbm, owner_ref),
+        (length_hbm, length_ref), (gain_hbm, gain_ref), (frames_hbm, frames_ref),
+    )
+    copies = [pltpu.make_async_copy(a, b, sems.at[i]) for i, (a, b) in enumerate(pairs)]
     for copy in copies:
         copy.start()
-    rows, width = frames_ref.shape
-    pieces = width // HD
-    chunk = cap * pieces
-    held[...] = jnp.zeros_like(held)
-    for o in range(owners):
-        count_ref[o] = 0
     for copy in copies:
         copy.wait()
-    first = lax.axis_index("sess") * rows
-    wide = frames_ref[...].astype(F32)
-    for r in range(rows):
-        o = owner_ref[session_ref[first + r]]
-        pair = count_ref[o]
-        count_ref[o] = pair + 1
-        for f in range(pieces):
-            held[pl.ds(o * chunk + pair * pieces + f, 1), :] = wide[r : r + 1, f * HD : (f + 1) * HD]
-    span = out_ref.shape[0] // owners
-    for o in range(owners):
-        piece = held[o * chunk : (o + 1) * chunk, :]
-        tile = jnp.concatenate([piece] * (16 // chunk), axis=0).astype(BF)
-        for k in range(span // 16):
-            out_ref[o * span + k * 16 : o * span + (k + 1) * 16, :] = tile
-    copy = pltpu.make_async_copy(out_ref, out_hbm, out_sem)
-    copy.start()
-    copy.wait()
-
-
-def table_kernel(
-    blocks, session_ref, owner_ref, length_ref, gain_ref,
-    collect_ref, place_ref, lane_length_ref, wide_gain_ref, target_ref,
-):
     wide_gain_ref[...] = gain_ref[...].astype(F32)
     sessions = session_ref.shape[1]
     slots, places = collect_ref.shape
-    me = lax.axis_index("sess")
+    blocks = chips * cores
+    chip, core = lax.axis_index("z"), lax.axis_index("core")
+    me = chip * cores + core
 
     def dot(a, b, dims):
         return lax.dot_general(
@@ -99,7 +74,8 @@
     same_block = (before // rows == after // rows) & (before < after)
     row_pair = dot(row_mine, one(same_block), ((1,), (0,)))[0:1].astype(I32)
     owned = row_mine[0:1] > 0.5
-    row_place = row_pair * blocks + iota((1, sessions), 1) // rows
+    row_block = iota((1, sessions), 1) // rows
+    row_place = row_pair * blocks + row_block % cores * chips + row_block // cores
     at_place = (iota((places, sessions), 0) == row_place) & owned
     at_slot = (iota((slots, sessions), 0) == row_slot) & owned
     collect_ref[...] = dot(one(at_slot), one(at_place), ((1,), (1,))).astype(BF)
@@ -112,13 +88,49 @@
     high = dot((length >> 4).astype(F32), lane_session, ((1,), (1,)))
     low = dot((length & 15).astype(F32), lane_session, ((1,), (1,)))
     lane_length_ref[...] = (high * 16.0 + low)[0:1].astype(I32)
-    local = (rows, sessions)
-    row_id = iota(local, 1)
-    own_id = me * rows + iota(local, 0)
-    own_owner = jnp.sum(jnp.where(row_id == own_id, row_owner, 0), axis=1, keepdims=True)
-    earlier = (row_id // rows == me) & (row_id < own_id) & (row_owner == own_owner)
-    own_pair = jnp.sum(jnp.where(earlier, 1, 0), axis=1, keepdims=True)
-    target_ref[...] = jnp.broadcast_to(own_pair * blocks + own_owner, target_ref.shape)
+
+    def local(block):
+        shape = (rows, sessions)
+        row_id = iota(shape, 1)
+        own_id = block * rows + iota(shape, 0)
+        own_owner = jnp.sum(jnp.where(row_id == own_id, row_owner, 0), axis=1, keepdims=True)
+        earlier = (row_id // rows == block) & (row_id < own_id) & (row_owner == own_owner)
+        return own_owner, jnp.sum(jnp.where(earlier, 1, 0), axis=1, keepdims=True)
+
+    for side in range(2):
+        source = jnp.where(side == 0, core, 1 - core)
+        owner, pair = local(chip * cores + source)
+        if side == 0:
+            target_ref[...] = jnp.broadcast_to(pair * blocks + owner, target_ref.shape)
+        line = (owner // cores * cores + source) * cap + pair
+        line = jnp.where(owner % cores == core, line, -1)
+        lanes = iota((rows, send_ref.shape[1]), 1)
+        send_ref[side * rows : (side + 1) * rows, :] = one(lanes == line).astype(BF)
+
+
+def dispatch_kernel(
+    chips, cores, cap, send_ref, frames_ref, other_ref, out_hbm, held, out_ref, sem
+):
+    rows, width = frames_ref.shape
+    pieces = width // HD
+    chunk = cores * cap * pieces
+    lines = lax.dot_general(
+        send_ref[:rows], frames_ref[...], (((0,), (0,)), ((), ())), preferred_element_type=F32
+    ) + lax.dot_general(
+        send_ref[rows:], other_ref[...], (((0,), (0,)), ((), ())), preferred_element_type=F32
+    )
+    lines = lines[: chips * cores * cap]
+    for f in range(pieces):
+        held[pl.ds(f, chips * cores * cap, stride=pieces), :] = lines[:, f * HD : (f + 1) * HD]
+    span = out_ref.shape[0] // chips
+    for z in range(chips):
+        piece = held[z * chunk : (z + 1) * chunk, :]
+        tile = jnp.concatenate([piece] * (16 // chunk), axis=0).astype(BF)
+        for k in range(span // 16):
+            out_ref[z * span + k * 16 : z * span + (k + 1) * 16, :] = tile
+    copy = pltpu.make_async_copy(out_ref, out_hbm, sem)
+    copy.start()
+    copy.wait()
 
 
 def turn(tiles):
@@ -136,43 +148,48 @@
 
 
 def attend_kernel(
-    owners, cap, pieces, x_ref, w_ref, collect_ref, place_ref, length_ref, gain_ref,
+    chips, cores, cap, pieces, x_ref, w_ref, collect_ref, place_ref, length_ref, gain_ref,
     kv_hbm, w_out_hbm, out_ref, kv_ref, w_out_ref, sems, exch_ref, rows_ref, score_ref, sum_ref,
 ):
+    key_copies = []
+    for i, first in enumerate(range(0, kv_ref.shape[1], KEY_BLOCK)):
+        at = pl.ds(first, min(KEY_BLOCK, kv_ref.shape[1] - first))
+        key_copies.append(pltpu.make_async_copy(kv_hbm.at[0, at], kv_ref.at[0, at], sems.at[2 + i]))
     copies = [
-        pltpu.make_async_copy(kv_hbm.at[0], kv_ref.at[0], sems.at[0]),
-        pltpu.make_async_copy(kv_hbm.at[1], kv_ref.at[1], sems.at[1]),
-        pltpu.make_async_copy(w_out_hbm, w_out_ref, sems.at[2]),
+        pltpu.make_async_copy(kv_hbm.at[1], kv_ref.at[1], sems.at[0]),
+        pltpu.make_async_copy(w_out_hbm, w_out_ref, sems.at[1]),
     ]
-    for copy in copies:
+    for copy in key_copies + copies:
         copy.start()
     places, model = rows_ref.shape
-    span = x_ref.shape[0] // owners
-    chunk = cap * pieces
+    owners = chips * cores
     tiles = model // HD
     context, slots = kv_ref.shape[1], kv_ref.shape[2]
     group = HD // slots
     steps = (context + group) // group
     half = steps // 2
-
+    span = x_ref.shape[0] // chips
+    chunk = cores * cap * pieces
+
+    def unpack(i, carry):
+        parts = []
+        for z in range(chips):
+            at = pl.multiple_of(z * span + i * 16, 16)
+            parts.append(x_ref[pl.ds(at, 16), :].astype(F32))
+        for b in range(2):
+            turned = turn([part[b * 8 : (b + 1) * 8] for part in parts])
+            for v, tile in enumerate(turned):
+                row = b * 8 + v
+                t, line = row // chunk, row % chunk // pieces
+                k = (i * (16 // chunk) + t) * pieces + row % pieces
+                first = line % cap * owners + line // cap * chips
+                exch_ref[k, first : first + chips, :] = tile
+        return carry
+
+    lax.fori_loop(0, span // 16, unpack, 0)
+    span = out_ref.shape[0] // owners
+    chunk = cap * pieces
     block = 16 // chunk
-
-    def unpack(i, carry):
-        for h in range(owners // 8):
-            parts = []
-            for o in range(8):
-                at = pl.multiple_of((h * 8 + o) * span + i * 16, 16)
-                parts.append(x_ref[pl.ds(at, 16), :].astype(F32))
-            for b in range(2):
-                turned = turn([part[b * 8 : (b + 1) * 8] for part in parts])
-                for v, tile in enumerate(turned):
-                    row = b * 8 + v
-                    t, j, f = row // chunk, row % chunk // pieces, row % pieces
-                    k = (i * block + t) * pieces + f
-                    exch_ref[k, j * owners + h * 8 : j * owners + h * 8 + 8, :] = tile
-        return carry
-
-    lax.fori_loop(0, span // 16, unpack, 0)
 
     squares = [jnp.zeros((places, HD), F32) for _ in range(2)]
     for k in range(tiles):
@@ -200,7 +217,7 @@
         sums[c % 2] += jnp.dot(stacked, both, preferred_element_type=F32)
     for i in range(2):
         sum_ref[2 + i] = sums[i]
-    live = lax.axis_index("sess") >= 0
+    live = lax.axis_index("core") >= 0
 
     @pl.when(live)
     def _():
@@ -213,9 +230,10 @@
         new_value = jnp.dot(collect, value, preferred_element_type=F32).astype(BF)
 
         own = iota((slots, HD), 0) == iota((slots, HD), 1) % slots
-        copies[0].wait()
         for g in range(half):
             first = 2 * g * group
+            if first % KEY_BLOCK == 0:
+                key_copies[first // KEY_BLOCK].wait()
             last = min(first + 2 * group, context)
             keys = kv_ref[0, first:last].reshape((last - first) * slots, HD)
             if last - first < 2 * group:
@@ -256,7 +274,7 @@
                 found = jnp.concatenate([found, new_value], axis=0)
             return found
 
-        copies[1].wait()
+        copies[0].wait()
         sums = [jnp.zeros((2 * places, deep), F32) for _ in range(2)]
         for c in range((half + 1) // 2):
             count = min(2, half - 2 * c)
@@ -277,7 +295,7 @@
         def _():
             total = sum_ref[0] + sum_ref[1]
             attended = (total[:places, :HD] + total[places:, HD:]).astype(BF)
-            copies[2].wait()
+            copies[1].wait()
             width = pieces * HD
             for i in range(span // 16):
                 found = [
@@ -288,20 +306,32 @@
                     )
                     for t in range(block)
                 ]
-                for h in range(owners // 8):
+                for h in range(cores):
                     turned = []
                     for b in range(2):
                         tiles_in = []
                         for v in range(8):
                             row = b * 8 + v
                             t, j, f = row // chunk, row % chunk // pieces, row % pieces
-                            first = j * owners + h * 8
-                            tiles_in.append(found[t][first : first + 8, f * HD : (f + 1) * HD])
+                            first = j * owners + h * chips
+                            tiles_in.append(found[t][first : first + chips, f * HD : (f + 1) * HD])
                         turned.append(turn(tiles_in))
-                    for o in range(8):
-                        at = (h * 8 + o) * span + i * 16
-                        both = jnp.concatenate([turned[0][o], turned[1][o]], axis=0)
+                    for z in range(chips):
+                        at = (z * cores + h) * span + i * 16
+                        both = jnp.concatenate([turned[0][z], turned[1][z]], axis=0)
                         out_ref[at : at + 16, :] = both.astype(BF)
+
+
+def attend_scratch(cache, w_out, exchange, tiles, places, model, steps):
+    return [
+        pltpu.VMEM(cache, BF),
+        pltpu.VMEM(w_out, BF),
+        pltpu.SemaphoreType.DMA((2 + pl.cdiv(cache[1], KEY_BLOCK),)),
+        pltpu.VMEM((tiles, places, HD), F32),
+        pltpu.VMEM((places, model), BF),
+        pltpu.VMEM((steps + (-steps) % 8, HD), F32),
+        pltpu.VMEM((4, 2 * places, 2 * HD), F32),
+    ]
 
 
 def finish_kernel(owners, cap, parts_ref, frames_ref, target_ref, out_ref, sums_ref):
@@ -330,13 +360,14 @@
         out_ref[:, cols] = (frames_ref[:, cols].astype(F32) + found[f]).astype(BF)
 
 
-def exchanged(array):
-    return lax.all_to_all(array, ("sess", "tp"), split_axis=0, concat_axis=0, tiled=True)
+def exchanged(array, axes):
+    return lax.all_to_all(array, axes, split_axis=0, concat_axis=0, tiled=True)
 
 
 def body(frames, norm_gain, w_qkv, w_out, kv_cache, frame_session, owner_of, context_len):
-    owners = lax.axis_size("sess")
+    chips, cores = lax.axis_size("z"), lax.axis_size("core")
     peers = lax.axis_size("tp")
+    owners = chips * cores
     rows, width = frames.shape
     slots = kv_cache.shape[1]
     cap = (slots + owners - 1) // owners
@@ -344,66 +375,59 @@
     pieces = width // HD
     exchange = (owners * peers * cap * pieces, HD)
 
+    other = lax.ppermute(frames, "core", [(c, c ^ 1) for c in range(cores)])
+    lists = [a.reshape(1, -1) for a in (frame_session, owner_of, context_len)]
+    gain = norm_gain.reshape(-1, HD)
+    *tables, target, send, frames_near = pl.pallas_call(
+        functools.partial(table_kernel, chips, cores, cap),
+        out_shape=(
+            pltpu.VMEM((slots, places), BF),
+            pltpu.VMEM((places, HD), F32),
+            pltpu.VMEM((1, HD), I32),
+            pltpu.VMEM(gain.shape, F32),
+            pltpu.VMEM((rows, HD), I32),
+            pltpu.VMEM((2 * rows, HD), BF),
+            pltpu.VMEM(frames.shape, frames.dtype),
+        ),
+        in_specs=[HBM] * 5,
+        out_specs=(VM,) * 7,
+        scratch_shapes=[
+            *[pltpu.VMEM(a.shape, a.dtype) for a in (*lists, gain)],
+            pltpu.SemaphoreType.DMA((5,)),
+        ],
+        compiler_params=limit(4),
+        cost_estimate=pl.CostEstimate(flops=10**9, bytes_accessed=10**6, transcendentals=0),
+        name="tables",
+    )(*far(*lists, gain, frames))
     outgoing = pl.pallas_call(
-        functools.partial(dispatch_kernel, owners, cap),
+        functools.partial(dispatch_kernel, chips, cores, cap),
         out_shape=pltpu.HBM(exchange, BF),
-        in_specs=[HBM, HBM, HBM],
+        in_specs=[VM] * 3,
         out_specs=HBM,
         scratch_shapes=[
-            pltpu.SMEM(frame_session.shape, I32),
-            pltpu.SMEM(owner_of.shape, I32),
-            pltpu.VMEM(frames.shape, BF),
             pltpu.VMEM((places * pieces, HD), F32),
             pltpu.VMEM(exchange, BF),
-            pltpu.SMEM((owners,), I32),
-            pltpu.SemaphoreType.DMA((3,)),
             pltpu.SemaphoreType.DMA,
         ],
         compiler_params=limit(4),
         name="dispatch",
-    )(*far(frame_session, owner_of, frames))
-    arrived = exchanged(outgoing)
-
-    tables = pl.pallas_call(
-        functools.partial(table_kernel, owners),
-        out_shape=(
-            pltpu.VMEM((slots, places), BF),
-            pltpu.VMEM((places, HD), F32),
-            pltpu.VMEM((1, HD), I32),
-            pltpu.VMEM((norm_gain.size // HD, HD), F32),
-            pltpu.VMEM((rows, HD), I32),
-        ),
-        in_specs=[VM] * 4,
-        out_specs=(VM,) * 5,
-        compiler_params=limit(4),
-        cost_estimate=pl.CostEstimate(flops=10**9, bytes_accessed=10**6, transcendentals=0),
-        name="tables",
-    )(
-        *[a.reshape(1, -1) for a in (frame_session, owner_of, context_len)],
-        norm_gain.reshape(-1, HD),
-    )
-    *tables, target = tables
+    )(*near(send, frames_near, other))
+    arrived = exchanged(outgoing, ("z", "tp"))
 
     cache = kv_cache.transpose(0, 2, 1, 3)
     steps = (cache.shape[1] + HD // slots) // (HD // slots)
     partial_rows = pl.pallas_call(
-        functools.partial(attend_kernel, owners, cap, pieces),
+        functools.partial(attend_kernel, chips, cores, cap, pieces),
         out_shape=pltpu.VMEM(exchange, BF),
         in_specs=[VM] * 6 + [HBM, HBM],
         out_specs=VM,
-        scratch_shapes=[
-            pltpu.VMEM(cache.shape, BF),
-            pltpu.VMEM(w_out.shape, BF),
-            pltpu.SemaphoreType.DMA((3,)),
-            pltpu.VMEM((peers * pieces, places, HD), F32),
-            pltpu.VMEM((places, peers * width), BF),
-            pltpu.VMEM((steps + (-steps) % 8, HD), F32),
-            pltpu.VMEM((4, 2 * places, 2 * HD), F32),
-        ],
+        scratch_shapes=attend_scratch(
+            cache.shape, w_out.shape, exchange, peers * pieces, places, peers * width, steps
+        ),
         compiler_params=limit(10),
         name="attend",
     )(*near(arrived, w_qkv, *tables), *far(cache, w_out))
-    parts = exchanged(partial_rows)
+    parts = exchanged(partial_rows, ("z", "core", "tp"))
     return pl.pallas_call(
         functools.partial(finish_kernel, owners, cap),
         out_shape=jax.ShapeDtypeStruct(frames.shape, frames.dtype),
@@ -412,19 +436,22 @@
         scratch_shapes=[pltpu.VMEM((places * pieces, HD), F32)],
         compiler_params=limit(4),
         name="finish",
-    )(*near(parts, frames, target))
+    )(*near(parts, frames_near, target))
 
 
 def solution(mesh):
+    sess, tp = mesh.shape["sess"], mesh.shape["tp"]
+    split = jax.sharding.Mesh(mesh.devices.reshape(sess // 2, 2, tp), ("z", "core", "tp"))
+    owner = ("z", "core")
     in_specs = (
-        P("sess", "tp"),
+        P(owner, "tp"),
         P(),
         P(None, None, "tp"),
         P("tp", None),
-        P(None, "sess", None, "tp"),
+        P(None, owner, None, "tp"),
         P(),
         P(),
         P(),
     )
-    out_specs = P("sess", "tp")
-    return jax.shard_map(body, mesh=mesh, in_specs=in_specs, out_specs=out_specs, check_vma=False)
+    out_specs = P(owner, "tp")
+    return jax.shard_map(body, mesh=split, in_specs=in_specs, out_specs=out_specs, check_vma=False)

time: 58.8 us -> 61.1 us (1.039)
  blocking collectives: 20.4 us -> 50.8 us
  starting transfers between devices: 15.7 us -> 3.2 us
  waiting for transfers between devices: 12.5 us -> 0.01 us
  local copies, waits for them, and re-layouts: 2.73 us -> 0.01 us
    all_to_all x1 -> x2, blocking collectives: 20.4 us -> 50.8 us  [exchanged(): return lax.all_to_all(array, axes, split_axis=0, concat_axis=0, tiled=True)]
    all_to_all x1 -> x0, starting transfers between devices: 15.7 us -> none  [exchanged(): lax.all_to_all(array, ('sess', 'tp'), split_axis=0, concat_axis=0, tiled=...]
    all_to_all x1 -> x0, waiting for transfers between devices: 12.5 us -> none  [exchanged(): lax.all_to_all(array, ('sess', 'tp'), split_axis=0, concat_axis=0, tiled=...]
    ppermute x0 -> x1, starting transfers between devices: none -> 3.2 us  [body(): other = lax.ppermute(frames, 'core', [(c, c ^ 1) for c in range(cores)])]
    unnamed x12 -> x2, local copies, waits for them, and re-layouts: 2.73 us -> 0.01 us
  transfers between devices with their start and end apart: 1 -> 1, of which waited for: 1 -> 0; matrix products, arithmetic and copies ran while one was open for 0% -> 0% of each run, Pallas kernels for 1% -> 2%
where the time goes in v5:
time: 61.1 us; the launch traced here: 60.9 us
  blocking collectives  50.8 us (83%)
  Pallas kernels  6.88 us (11%)
  starting transfers between devices  3.2 us (5%)
    all_to_all x2, blocking collectives, exchanged(): return lax.all_to_all(array, axes, split_axis=0, concat_axis=0, tiled=True)  50.8 us
    pallas_call x1, Pallas kernels, body(): pl.pallas_call(functools.partial(attend_kernel, chips, cores, cap, pieces...  4.02 us
    ppermute x1, starting transfers between devices, body(): other = lax.ppermute(frames, 'core', [(c, c ^ 1) for c in range(cores)])  3.2 us
    pallas_call x1, Pallas kernels, body(): pl.pallas_call(functools.partial(table_kernel, chips, cores, cap), out_sh...  1.28 us
  transfers between devices with their start and end apart: 1, of which 0 were waited for; matrix products, arithmetic and copies ran while one was open for 0% of the time, Pallas kernels for 2%

profile of v5, /device:TPU:1, one launch (start us, length us, event | category | flops | bytes accessed | tf_op | source)
XLA Modules:
  0.0 60.9 jit_solution(1184828503717005444)
XLA Ops:
  0.0 0.0 copy-start
  0.0 3.2 %collective-permute-start = (bf16[16,256]{1,0:T(8,128)(2,1)}, bf16[16,256]{1,0:T(8,128)(2,1)S(1)}, u32[]{:S(2)}, u32[]{:S(2)}) collective-permute-start(bf16[16,256]{1,0:T(8,128)(2,1)} %frames_hbm.1), channel_id=1, source_target_pairs={{0,16},{16,0},{1,17},{17,1},{2,18},{18,2},{3,19},{19,3},{4,20},{20... | collective-permute-start | bytes 24584 | tf_op jit(solution)/shard_map/ppermute | solution.py:378
  3.2 1.3 %tables.1 = (bf16[32,32]{1,0:T(8,128)(2,1)S(1)}, f32[32,128]{1,0:T(8,128)S(1)}, s32[1,128]{1,0:T(1,128)S(1)}, f32[32,128]{1,0:T(8,128)S(1)}, s32[16,128]{1,0:T(8...) custom-call(s32[1,256]{1,0:T(1,128)} %bitcast.15, s32[1,256]{1,0:T(1,128)} %bitcast.16, ...), custom_call_target="tpu_custom_call" | custom-call | flops 1000000000 | bytes 1000000 | tf_op jit(solution)/shard_map/tables/pallas_call | solution.py:381
  4.5 0.0 collective-permute-done.other_ref
  4.5 0.9 %dispatch.1 = bf16[1024,128]{1,0:T(8,128)(2,1)} custom-call(bf16[32,128]{1,0:T(8,128)(2,1)S(1)} %get-tuple-element.12.send_ref, bf16[16,256]{1,0:T(8,128)(2,1)S(1)} %get-tuple-element.13.frames_ref, bf16[16,256]{1,0:T(8,128)(2,1)S(1)} %collective-permute-done.other_ref), custom_call_target="tpu_custom_call" | custom-call | tf_op jit(solution)/shard_map/dispatch/pallas_call | solution.py:402
  5.4 28.2 %all_to_all.22 = bf16[128,8,128]{2,1,0:T(8,128)(2,1)S(1)} all-to-all(bf16[128,8,128]{2,1,0:T(8,128)(2,1)} %bitcast.13), channel_id=1, replica_groups=mesh['z'=8,'core'=2,'tp'=16] {'z','tp'}, dimensions={0} | all-to-all | bytes 524288 | tf_op jit(solution)/shard_map/all_to_all | solution.py:364
  33.7 0.0 copy-done
  33.7 4.0 %attend.1 = bf16[1024,128]{1,0:T(8,128)(2,1)S(1)} custom-call(bf16[1024,128]{1,0:T(8,128)(2,1)S(1)} %bitcast.9, bf16[3,4096,128]{2,1,0:T(8,128)(2,1)S(1)} %copy-done, bf16[32,32]{1,0:T(8,128)(2,1)S(1)} %get-tuple-element.14.collect_ref, f32[32,128]{1,0:T(8,128)S(1)} %get-tuple-element.15.place_ref, s32[1,128]{1,0:T(1,128)S(1)} %get-tuple-element.16.length_ref, ...), custom_call_target="tpu_custom_call" | custom-call | tf_op jit(solution)/shard_map/attend/pallas_call | solution.py:419
  37.7 22.5 %all_to_all.23 = bf16[256,4,128]{2,1,0:T(4,128)(2,1)S(1)} all-to-all(bf16[256,4,128]{2,1,0:T(4,128)(2,1)S(1)} %bitcast.10), channel_id=1, replica_groups=mesh['z'=8,'core'=2,'tp'=16] {'z','core','tp'}, dimensions={0} | all-to-all | bytes 524288 | tf_op jit(solution)/shard_map/all_to_all | solution.py:364
  60.2 0.7 %finish.1 = bf16[16,256]{1,0:T(8,128)(2,1)} custom-call(bf16[1024,128]{1,0:T(8,128)(2,1)S(1)} %bitcast.11, bf16[16,256]{1,0:T(8,128)(2,1)S(1)} %get-tuple-element.13.frames_ref, s32[16,128]{1,0:T(8,128)S(1)} %get-tuple-element.18.target_ref), custom_call_target="tpu_custom_call" | custom-call | tf_op jit(solution)/shard_map/finish/pallas_call | solution.py:431
Async XLA Ops:
  0.0 33.7 %copy-start = (bf16[3,4096,128]{2,1,0:T(8,128)(2,1)S(1)}, bf16[3,4096,128]{2,1,0:T(8,128)(2,1)}, u32[]{:S(2)}) copy-start(bf16[3,4096,128]{2,1,0:T(8,128)(2,1)} %w_ref.1) | copy-start | bytes 9437188
  0.0 4.5 %collective-permute-start = (bf16[16,256]{1,0:T(8,128)(2,1)}, bf16[16,256]{1,0:T(8,128)(2,1)S(1)}, u32[]{:S(2)}, u32[]{:S(2)}) collective-permute-start(bf16[16,256]{1,0:T(8,128)(2,1)} %frames_hbm.1), channel_id=1, source_target_pairs={{0,16},{16,0},{1,17},{17,1},{2,18},{18,2},{3,19},{19,3},{4,20},{20... | collective-permute-start | bytes 24584 | tf_op jit(solution)/shard_map/ppermute | solution.py:378

commit v6 on v4

--- a/solution.py
+++ b/solution.py
@@ -8,6 +8,7 @@
 from jax.sharding import PartitionSpec as P
 
 HD = 128
+KEY_BLOCK = 192
 BF = jnp.bfloat16
 F32 = jnp.float32
 I32 = jnp.int32
@@ -33,7 +34,7 @@
 
 def dispatch_kernel(
     owners, cap, session_hbm, owner_hbm, frames_hbm, out_hbm,
-    session_ref, owner_ref, frames_ref, held, out_ref, count_ref, in_sems, out_sem,
+    session_ref, owner_ref, frames_ref, held, out_ref, count_ref, in_sems, out_sems,
 ):
     copies = [
         pltpu.make_async_copy(session_hbm, session_ref, in_sems.at[0]),
@@ -59,14 +60,20 @@
         for f in range(pieces):
             held[pl.ds(o * chunk + pair * pieces + f, 1), :] = wide[r : r + 1, f * HD : (f + 1) * HD]
     span = out_ref.shape[0] // owners
+    parts = out_sems.shape[0]
+    sent = []
     for o in range(owners):
         piece = held[o * chunk : (o + 1) * chunk, :]
         tile = jnp.concatenate([piece] * (16 // chunk), axis=0).astype(BF)
         for k in range(span // 16):
             out_ref[o * span + k * 16 : o * span + (k + 1) * 16, :] = tile
-    copy = pltpu.make_async_copy(out_ref, out_hbm, out_sem)
-    copy.start()
-    copy.wait()
+        if (o + 1) % (owners // parts) == 0:
+            at = pl.ds((o + 1 - owners // parts) * span, owners // parts * span)
+            copy = pltpu.make_async_copy(out_ref.at[at], out_hbm.at[at], out_sems.at[o // (owners // parts)])
+            copy.start()
+            sent.append(copy)
+    for copy in sent:
+        copy.wait()
 
 
 def table_kernel(
@@ -139,12 +146,15 @@
     owners, cap, pieces, x_ref, w_ref, collect_ref, place_ref, length_ref, gain_ref,
     kv_hbm, w_out_hbm, out_ref, kv_ref, w_out_ref, sems, exch_ref, rows_ref, score_ref, sum_ref,
 ):
+    key_copies = []
+    for i, first in enumerate(range(0, kv_ref.shape[1], KEY_BLOCK)):
+        at = pl.ds(first, min(KEY_BLOCK, kv_ref.shape[1] - first))
+        key_copies.append(pltpu.make_async_copy(kv_hbm.at[0, at], kv_ref.at[0, at], sems.at[2 + i]))
     copies = [
-        pltpu.make_async_copy(kv_hbm.at[0], kv_ref.at[0], sems.at[0]),
-        pltpu.make_async_copy(kv_hbm.at[1], kv_ref.at[1], sems.at[1]),
-        pltpu.make_async_copy(w_out_hbm, w_out_ref, sems.at[2]),
+        pltpu.make_async_copy(kv_hbm.at[1], kv_ref.at[1], sems.at[0]),
+        pltpu.make_async_copy(w_out_hbm, w_out_ref, sems.at[1]),
     ]
-    for copy in copies:
+    for copy in key_copies + copies:
         copy.start()
     places, model = rows_ref.shape
     span = x_ref.shape[0] // owners
@@ -213,9 +223,10 @@
         new_value = jnp.dot(collect, value, preferred_element_type=F32).astype(BF)
 
         own = iota((slots, HD), 0) == iota((slots, HD), 1) % slots
-        copies[0].wait()
         for g in range(half):
             first = 2 * g * group
+            if first % KEY_BLOCK == 0:
+                key_copies[first // KEY_BLOCK].wait()
             last = min(first + 2 * group, context)
             keys = kv_ref[0, first:last].reshape((last - first) * slots, HD)
             if last - first < 2 * group:
@@ -256,7 +267,7 @@
                 found = jnp.concatenate([found, new_value], axis=0)
             return found
 
-        copies[1].wait()
+        copies[0].wait()
         sums = [jnp.zeros((2 * places, deep), F32) for _ in range(2)]
         for c in range((half + 1) // 2):
             count = min(2, half - 2 * c)
@@ -277,7 +288,7 @@
         def _():
             total = sum_ref[0] + sum_ref[1]
             attended = (total[:places, :HD] + total[places:, HD:]).astype(BF)
-            copies[2].wait()
+            copies[1].wait()
             width = pieces * HD
             for i in range(span // 16):
                 found = [
@@ -304,6 +315,18 @@
                         out_ref[at : at + 16, :] = both.astype(BF)
 
 
+def attend_scratch(cache, w_out, exchange, tiles, places, model, steps):
+    return [
+        pltpu.VMEM(cache, BF),
+        pltpu.VMEM(w_out, BF),
+        pltpu.SemaphoreType.DMA((2 + pl.cdiv(cache[1], KEY_BLOCK),)),
+        pltpu.VMEM((tiles, places, HD), F32),
+        pltpu.VMEM((places, model), BF),
+        pltpu.VMEM((steps + (-steps) % 8, HD), F32),
+        pltpu.VMEM((4, 2 * places, 2 * HD), F32),
+    ]
+
+
 def finish_kernel(owners, cap, parts_ref, frames_ref, target_ref, out_ref, sums_ref):
     rows, width = frames_ref.shape
     pieces = width // HD
@@ -357,7 +380,7 @@
             pltpu.VMEM(exchange, BF),
             pltpu.SMEM((owners,), I32),
             pltpu.SemaphoreType.DMA((3,)),
-            pltpu.SemaphoreType.DMA,
+            pltpu.SemaphoreType.DMA((4,)),
         ],
         compiler_params=limit(4),
         name="dispatch",
@@ -391,15 +414,9 @@
         out_shape=pltpu.VMEM(exchange, BF),
         in_specs=[VM] * 6 + [HBM, HBM],
         out_specs=VM,
-        scratch_shapes=[
-            pltpu.VMEM(cache.shape, BF),
-            pltpu.VMEM(w_out.shape, BF),
-            pltpu.SemaphoreType.DMA((3,)),
-            pltpu.VMEM((peers * pieces, places, HD), F32),
-            pltpu.VMEM((places, peers * width), BF),
-            pltpu.VMEM((steps + (-steps) % 8, HD), F32),
-            pltpu.VMEM((4, 2 * places, 2 * HD), F32),
-        ],
+        scratch_shapes=attend_scratch(
+            cache.shape, w_out.shape, exchange, peers * pieces, places, peers * width, steps
+        ),
         compiler_params=limit(10),
         name="attend",
     )(*near(arrived, w_qkv, *tables), *far(cache, w_out))

time: 58.8 us -> 58.5 us (level)
  no operation moved by 1% of the time
where the time goes in v6:
time: 58.5 us; the launch traced here: 58.1 us
  blocking collectives  20.4 us (35%)
  starting transfers between devices  15.7 us (27%)
  waiting for transfers between devices  12.5 us (21%)
  Pallas kernels  6.84 us (12%)
  local copies, waits for them, and re-layouts  2.73 us (5%)
    all_to_all x1, blocking collectives, exchanged(): lax.all_to_all(array, ('sess', 'tp'), split_axis=0, concat_axis=0, tiled=...  20.4 us
    all_to_all x1, starting transfers between devices, exchanged(): lax.all_to_all(array, ('sess', 'tp'), split_axis=0, concat_axis=0, tiled=...  15.7 us
    all_to_all x1, waiting for transfers between devices, exchanged(): lax.all_to_all(array, ('sess', 'tp'), split_axis=0, concat_axis=0, tiled=...  12.5 us
    pallas_call x1, Pallas kernels, body(): pl.pallas_call(functools.partial(attend_kernel, owners, cap, pieces), out...  4.03 us
    unnamed x12, local copies, waits for them, and re-layouts  2.73 us
    pallas_call x1, Pallas kernels, body(): pl.pallas_call(functools.partial(dispatch_kernel, owners, cap), out_shape...  1.68 us
  transfers between devices with their start and end apart: 1, of which 1 were waited for; matrix products, arithmetic and copies ran while one was open for 0% of the time, Pallas kernels for 1%

profile of v6, /device:TPU:1, one launch (start us, length us, event | category | flops | bytes accessed | tf_op | source)
XLA Modules:
  0.0 58.1 jit_solution(8207128191906648697)
XLA Ops:
  0.0 0.0 copy-start
  0.0 1.7 %dispatch.1 = bf16[1024,128]{1,0:T(8,128)(2,1)} custom-call(s32[256]{0:T(256)} %session_hbm.1, s32[256]{0:T(256)} %owner_hbm.1, bf16[16,256]{1,0:T(8,128)(2,1)} %frames_ref.1), custom_call_target="tpu_custom_call" | custom-call | tf_op jit(solution)/shard_map/dispatch/pallas_call | solution.py:370
  1.7 15.7 %all-to-all-start = ((bf16[256,4,128]{2,1,0:T(4,128)(2,1)}), bf16[256,4,128]{2,1,0:T(4,128)(2,1)S(1)}, u32[]{:S(2)}, u32[]{:S(2)}) async-start(bf16[256,4,128]{2,1,0:T(4,128)(2,1)} %bitcast.17), calls=%async_computation | async-start | bytes 524288 | tf_op jit(solution)/shard_map/all_to_all | solution.py:357
  17.4 0.0 copy-start.2
  17.4 0.7 %copy-done.2 = s32[256]{0:T(256)S(1)} copy-done((s32[256]{0:T(256)S(1)}, s32[256]{0:T(256)}, u32[]{:S(2)}) %copy-start.2) | copy-done | bytes 1048
  18.0 0.0 copy-start.3
  18.0 0.7 %copy-done.3 = s32[256]{0:T(256)S(1)} copy-done((s32[256]{0:T(256)S(1)}, s32[256]{0:T(256)}, u32[]{:S(2)}) %copy-start.3) | copy-done | bytes 1048
  18.7 0.0 copy-start.4
  18.7 0.7 %copy-done.4 = bf16[4096]{0:T(1024)(128)(2,1)S(1)} copy-done((bf16[4096]{0:T(1024)(128)(2,1)S(1)}, bf16[4096]{0:T(1024)(128)(2,1)}, u32[]{:S(2)}) %copy-start.4) | copy-done | bytes 8216
  19.4 0.0 copy-start.5
  19.4 0.7 %copy-done.5 = s32[256]{0:T(256)S(1)} copy-done((s32[256]{0:T(256)S(1)}, s32[256]{0:T(256)}, u32[]{:S(2)}) %copy-start.5) | copy-done | bytes 1048
  20.1 0.5 tables.1
  20.6 0.0 copy-start.1
  20.6 12.5 %all-to-all-done = bf16[256,4,128]{2,1,0:T(4,128)(2,1)S(1)} async-done(((bf16[256,4,128]{2,1,0:T(4,128)(2,1)}), bf16[256,4,128]{2,1,0:T(4,128)(2,1)S(1)}, u32[]{:S(2)}, u32[]{:S(2)}) %all-to-all-start) | async-done | bytes 262176 | tf_op jit(solution)/shard_map/all_to_all | solution.py:357
  33.1 0.0 copy-done
  33.1 4.0 %attend.1 = bf16[1024,128]{1,0:T(8,128)(2,1)S(1)} custom-call(bf16[1024,128]{1,0:T(8,128)(2,1)S(1)} %bitcast.9, bf16[3,4096,128]{2,1,0:T(8,128)(2,1)S(1)} %copy-done, bf16[32,32]{1,0:T(8,128)(2,1)S(1)} %get-tuple-element.10.collect_ref, f32[32,128]{1,0:T(8,128)S(1)} %get-tuple-element.11.place_ref, s32[1,128]{1,0:T(1,128)S(1)} %get-tuple-element.12.length_ref, ...), custom_call_target="tpu_custom_call" | custom-call | tf_op jit(solution)/shard_map/attend/pallas_call | solution.py:412
  37.1 20.4 %all_to_all.22 = bf16[256,4,128]{2,1,0:T(4,128)(2,1)S(1)} all-to-all(bf16[256,4,128]{2,1,0:T(4,128)(2,1)S(1)} %bitcast.10), channel_id=1, replica_groups=mesh['sess'=16,'tp'=16] {'sess','tp'}, dimensions={0} | all-to-all | bytes 524288 | tf_op jit(solution)/shard_map/all_to_all | solution.py:357
  57.5 0.0 copy-done.1
  57.5 0.7 %finish.1 = bf16[16,256]{1,0:T(8,128)(2,1)} custom-call(bf16[1024,128]{1,0:T(8,128)(2,1)S(1)} %bitcast.11, bf16[16,256]{1,0:T(8,128)(2,1)S(1)} %copy-done.1, s32[16,128]{1,0:T(8,128)S(1)} %get-tuple-element.14.target_ref), custom_call_target="tpu_custom_call" | custom-call | tf_op jit(solution)/shard_map/finish/pallas_call | solution.py:424
Async XLA Ops:
  0.0 33.1 %copy-start = (bf16[3,4096,128]{2,1,0:T(8,128)(2,1)S(1)}, bf16[3,4096,128]{2,1,0:T(8,128)(2,1)}, u32[]{:S(2)}) copy-start(bf16[3,4096,128]{2,1,0:T(8,128)(2,1)} %w_ref.1) | copy-start | bytes 9437188
  1.7 31.4 %all-to-all-start = ((bf16[256,4,128]{2,1,0:T(4,128)(2,1)}), bf16[256,4,128]{2,1,0:T(4,128)(2,1)S(1)}, u32[]{:S(2)}, u32[]{:S(2)}) async-start(bf16[256,4,128]{2,1,0:T(4,128)(2,1)} %bitcast.17), calls=%async_computation | async-start | bytes 524288 | tf_op jit(solution)/shard_map/all_to_all | solution.py:357
  17.4 0.7 %copy-start.2 = (s32[256]{0:T(256)S(1)}, s32[256]{0:T(256)}, u32[]{:S(2)}) copy-start(s32[256]{0:T(256)} %session_hbm.1) | copy-start | bytes 3076
  18.0 0.7 %copy-start.3 = (s32[256]{0:T(256)S(1)}, s32[256]{0:T(256)}, u32[]{:S(2)}) copy-start(s32[256]{0:T(256)} %owner_hbm.1) | copy-start | bytes 3076
  18.7 0.7 %copy-start.4 = (bf16[4096]{0:T(1024)(128)(2,1)S(1)}, bf16[4096]{0:T(1024)(128)(2,1)}, u32[]{:S(2)}) copy-start(bf16[4096]{0:T(1024)(128)(2,1)} %param.9) | copy-start | bytes 24580
  19.4 0.7 %copy-start.5 = (s32[256]{0:T(256)S(1)}, s32[256]{0:T(256)}, u32[]{:S(2)}) copy-start(s32[256]{0:T(256)} %param.15) | copy-start | bytes 3076
  20.6 36.9 %copy-start.1 = (bf16[16,256]{1,0:T(8,128)(2,1)S(1)}, bf16[16,256]{1,0:T(8,128)(2,1)}, u32[]{:S(2)}) copy-start(bf16[16,256]{1,0:T(8,128)(2,1)} %frames_ref.1) | copy-start | bytes 24580

commit v7 on v6

--- a/solution.py
+++ b/solution.py
@@ -33,14 +33,17 @@
 
 
 def dispatch_kernel(
-    owners, cap, session_hbm, owner_hbm, frames_hbm, out_hbm,
-    session_ref, owner_ref, frames_ref, held, out_ref, count_ref, in_sems, out_sems,
+    owners, cap, session_hbm, owner_hbm, frames_hbm, session_row, owner_row, length_row, gain_hbm,
+    out_hbm, collect_ref, place_ref, lane_length_ref, wide_gain_ref, target_ref, frames_ref,
+    session_ref, owner_ref, session_near, owner_near, length_near, gain_near,
+    held, out_ref, count_ref, in_sems, out_sems,
 ):
-    copies = [
-        pltpu.make_async_copy(session_hbm, session_ref, in_sems.at[0]),
-        pltpu.make_async_copy(owner_hbm, owner_ref, in_sems.at[1]),
-        pltpu.make_async_copy(frames_hbm, frames_ref, in_sems.at[2]),
-    ]
+    pairs = (
+        (session_hbm, session_ref), (owner_hbm, owner_ref), (frames_hbm, frames_ref),
+        (session_row, session_near), (owner_row, owner_near), (length_row, length_near),
+        (gain_hbm, gain_near),
+    )
+    copies = [pltpu.make_async_copy(a, b, in_sems.at[i]) for i, (a, b) in enumerate(pairs)]
     for copy in copies:
         copy.start()
     rows, width = frames_ref.shape
@@ -72,11 +75,18 @@
             copy = pltpu.make_async_copy(out_ref.at[at], out_hbm.at[at], out_sems.at[o // (owners // parts)])
             copy.start()
             sent.append(copy)
-    for copy in sent:
-        copy.wait()
-
-
-def table_kernel(
+
+    @pl.when(lax.axis_index("sess") >= 0)
+    def _():
+        write_tables(
+            owners, session_near, owner_near, length_near, gain_near,
+            collect_ref, place_ref, lane_length_ref, wide_gain_ref, target_ref,
+        )
+        for copy in sent:
+            copy.wait()
+
+
+def write_tables(
     blocks, session_ref, owner_ref, length_ref, gain_ref,
     collect_ref, place_ref, lane_length_ref, wide_gain_ref, target_ref,
 ):
@@ -367,45 +377,36 @@
     pieces = width // HD
     exchange = (owners * peers * cap * pieces, HD)
 
-    outgoing = pl.pallas_call(
+    lists = [a.reshape(1, -1) for a in (frame_session, owner_of, context_len)]
+    lists.append(norm_gain.reshape(-1, HD))
+    outgoing, *tables, target, frames_near = pl.pallas_call(
         functools.partial(dispatch_kernel, owners, cap),
-        out_shape=pltpu.HBM(exchange, BF),
-        in_specs=[HBM, HBM, HBM],
-        out_specs=HBM,
-        scratch_shapes=[
-            pltpu.SMEM(frame_session.shape, I32),
-            pltpu.SMEM(owner_of.shape, I32),
-            pltpu.VMEM(frames.shape, BF),
-            pltpu.VMEM((places * pieces, HD), F32),
-            pltpu.VMEM(exchange, BF),
-            pltpu.SMEM((owners,), I32),
-            pltpu.SemaphoreType.DMA((3,)),
-            pltpu.SemaphoreType.DMA((4,)),
-        ],
-        compiler_params=limit(4),
-        name="dispatch",
-    )(*far(frame_session, owner_of, frames))
-    arrived = exchanged(outgoing)
-
-    tables = pl.pallas_call(
-        functools.partial(table_kernel, owners),
         out_shape=(
+            pltpu.HBM(exchange, BF),
             pltpu.VMEM((slots, places), BF),
             pltpu.VMEM((places, HD), F32),
             pltpu.VMEM((1, HD), I32),
             pltpu.VMEM((norm_gain.size // HD, HD), F32),
             pltpu.VMEM((rows, HD), I32),
+            pltpu.VMEM(frames.shape, frames.dtype),
         ),
-        in_specs=[VM] * 4,
-        out_specs=(VM,) * 5,
+        in_specs=[HBM] * 7,
+        out_specs=(HBM,) + (VM,) * 6,
+        scratch_shapes=[
+            pltpu.SMEM(frame_session.shape, I32),
+            pltpu.SMEM(owner_of.shape, I32),
+            *[pltpu.VMEM(a.shape, a.dtype) for a in lists],
+            pltpu.VMEM((places * pieces, HD), F32),
+            pltpu.VMEM(exchange, BF),
+            pltpu.SMEM((owners,), I32),
+            pltpu.SemaphoreType.DMA((7,)),
+            pltpu.SemaphoreType.DMA((4,)),
+        ],
         compiler_params=limit(4),
-        cost_estimate=pl.CostEstimate(flops=10**9, bytes_accessed=10**6, transcendentals=0),
-        name="tables",
-    )(
-        *[a.reshape(1, -1) for a in (frame_session, owner_of, context_len)],
-        norm_gain.reshape(-1, HD),
-    )
-    *tables, target = tables
+        cost_estimate=pl.CostEstimate(flops=10**9, bytes_accessed=10**7, transcendentals=0),
+        name="dispatch",
+    )(*far(frame_session, owner_of, frames, *lists))
+    arrived = exchanged(outgoing)
 
     cache = kv_cache.transpose(0, 2, 1, 3)
     steps = (cache.shape[1] + HD // slots) // (HD // slots)
@@ -429,7 +430,7 @@
         scratch_shapes=[pltpu.VMEM((places * pieces, HD), F32)],
         compiler_params=limit(4),
         name="finish",
-    )(*near(parts, frames, target))
+    )(*near(parts, frames_near, target))
 
 
 def solution(mesh):

time: 58.5 us -> 58.4 us (level)
  blocking collectives: 20.4 us -> 51.8 us
  starting transfers between devices: 15.7 us -> 0 us
  waiting for transfers between devices: 12.5 us -> 0 us
  local copies, waits for them, and re-layouts: 2.73 us -> 0.01 us
    all_to_all x1 -> x2, blocking collectives: 20.4 us -> 51.8 us  [exchanged(): lax.all_to_all(array, ('sess', 'tp'), split_axis=0, concat_axis=0, tiled=...]
    all_to_all x1 -> x0, starting transfers between devices: 15.7 us -> none  [exchanged(): lax.all_to_all(array, ('sess', 'tp'), split_axis=0, concat_axis=0, tiled=...]
    all_to_all x1 -> x0, waiting for transfers between devices: 12.5 us -> none  [exchanged(): lax.all_to_all(array, ('sess', 'tp'), split_axis=0, concat_axis=0, tiled=...]
    unnamed x12 -> x2, local copies, waits for them, and re-layouts: 2.73 us -> 0.01 us
  transfers between devices with their start and end apart: 1 -> 0, of which waited for: 1 -> 0; matrix products, arithmetic and copies ran while one was open for 0% -> 0% of each run, Pallas kernels for 1% -> 0%
where the time goes in v7:
time: 58.4 us; the launch traced here: 58.2 us
  blocking collectives  51.8 us (89%)
  Pallas kernels  6.41 us (11%)
    all_to_all x2, blocking collectives, exchanged(): lax.all_to_all(array, ('sess', 'tp'), split_axis=0, concat_axis=0, tiled=...  51.8 us
    pallas_call x1, Pallas kernels, body(): pl.pallas_call(functools.partial(attend_kernel, owners, cap, pieces), out...  4.02 us
    pallas_call x1, Pallas kernels, body(): pl.pallas_call(functools.partial(dispatch_kernel, owners, cap), out_shape...  1.72 us

profile of v7, /device:TPU:1, one launch (start us, length us, event | category | flops | bytes accessed | tf_op | source)
XLA Modules:
  0.0 58.2 jit_solution(16075702423303147997)
XLA Ops:
  0.0 0.0 copy-start
  0.0 1.7 %dispatch.1 = (bf16[1024,128]{1,0:T(8,128)(2,1)}, bf16[32,32]{1,0:T(8,128)(2,1)S(1)}, f32[32,128]{1,0:T(8,128)S(1)}, s32[1,128]{1,0:T(1,128)S(1)}, f32[32,128]{1...) custom-call(s32[256]{0:T(256)} %session_hbm.1, s32[256]{0:T(256)} %owner_hbm.1, ...), custom_call_target="tpu_custom_call" | custom-call | flops 1000000000 | bytes 10000000 | tf_op jit(solution)/shard_map/dispatch/pallas_call | solution.py:382
  1.7 31.4 %all_to_all.22 = bf16[256,4,128]{2,1,0:T(4,128)(2,1)S(1)} all-to-all(bf16[256,4,128]{2,1,0:T(4,128)(2,1)} %bitcast.13), channel_id=1, replica_groups=mesh['sess'=16,'tp'=16] {'sess','tp'}, dimensions={0} | all-to-all | bytes 524288 | tf_op jit(solution)/shard_map/all_to_all | solution.py:367
  33.1 0.0 copy-done
  33.1 4.0 %attend.1 = bf16[1024,128]{1,0:T(8,128)(2,1)S(1)} custom-call(bf16[1024,128]{1,0:T(8,128)(2,1)S(1)} %bitcast.9, bf16[3,4096,128]{2,1,0:T(8,128)(2,1)S(1)} %copy-done, bf16[32,32]{1,0:T(8,128)(2,1)S(1)} %get-tuple-element.13.collect_ref, f32[32,128]{1,0:T(8,128)S(1)} %get-tuple-element.14.place_ref, s32[1,128]{1,0:T(1,128)S(1)} %get-tuple-element.15.length_ref, ...), custom_call_target="tpu_custom_call" | custom-call | tf_op jit(solution)/shard_map/attend/pallas_call | solution.py:413
  37.1 20.4 %all_to_all.23 = bf16[256,4,128]{2,1,0:T(4,128)(2,1)S(1)} all-to-all(bf16[256,4,128]{2,1,0:T(4,128)(2,1)S(1)} %bitcast.10), channel_id=1, replica_groups=mesh['sess'=16,'tp'=16] {'sess','tp'}, dimensions={0} | all-to-all | bytes 524288 | tf_op jit(solution)/shard_map/all_to_all | solution.py:367
  57.5 0.7 %finish.1 = bf16[16,256]{1,0:T(8,128)(2,1)} custom-call(bf16[1024,128]{1,0:T(8,128)(2,1)S(1)} %bitcast.11, bf16[16,256]{1,0:T(8,128)(2,1)S(1)} %get-tuple-element.17.frames_ref, s32[16,128]{1,0:T(8,128)S(1)} %get-tuple-element.18.target_ref), custom_call_target="tpu_custom_call" | custom-call | tf_op jit(solution)/shard_map/finish/pallas_call | solution.py:425
Async XLA Ops:
  0.0 33.1 %copy-start = (bf16[3,4096,128]{2,1,0:T(8,128)(2,1)S(1)}, bf16[3,4096,128]{2,1,0:T(8,128)(2,1)}, u32[]{:S(2)}) copy-start(bf16[3,4096,128]{2,1,0:T(8,128)(2,1)} %w_ref.1) | copy-start | bytes 9437188

commit v8 on v7

--- a/solution.py
+++ b/solution.py
@@ -164,7 +164,7 @@
         pltpu.make_async_copy(kv_hbm.at[1], kv_ref.at[1], sems.at[0]),
         pltpu.make_async_copy(w_out_hbm, w_out_ref, sems.at[1]),
     ]
-    for copy in key_copies + copies:
+    for copy in key_copies:
         copy.start()
     places, model = rows_ref.shape
     span = x_ref.shape[0] // owners
@@ -177,8 +177,11 @@
 
     block = 16 // chunk
 
+    halves = owners // 8
+
     def unpack(i, carry):
-        for h in range(owners // 8):
+        sums = list(carry)
+        for h in range(halves):
             parts = []
             for o in range(8):
                 at = pl.multiple_of((h * 8 + o) * span + i * 16, 16)
@@ -190,15 +193,12 @@
                     t, j, f = row // chunk, row % chunk // pieces, row % pieces
                     k = (i * block + t) * pieces + f
                     exch_ref[k, j * owners + h * 8 : j * owners + h * 8 + 8, :] = tile
-        return carry
-
-    lax.fori_loop(0, span // 16, unpack, 0)
-
-    squares = [jnp.zeros((places, HD), F32) for _ in range(2)]
-    for k in range(tiles):
-        part = exch_ref[k]
-        squares[k % 2] += part * part
-    scale = lax.rsqrt(jnp.sum(squares[0] + squares[1], axis=1, keepdims=True) / model + 1e-05)
+                    sums[j * halves + h] += tile * tile
+        return tuple(sums)
+
+    squares = tuple(jnp.zeros((8, HD), F32) for _ in range(cap * halves))
+    squares = jnp.concatenate(lax.fori_loop(0, span // 16, unpack, squares), axis=0)
+    scale = lax.rsqrt(jnp.sum(squares, axis=1, keepdims=True) / model + 1e-05)
     for k in range(tiles):
         cols = slice(k * HD, (k + 1) * HD)
         rows_ref[:, cols] = (exch_ref[k] * scale * gain_ref[k : k + 1, :]).astype(BF)
@@ -221,6 +221,8 @@
     for i in range(2):
         sum_ref[2 + i] = sums[i]
     live = lax.axis_index("sess") >= 0
+    for copy in copies:
+        copy.start()
 
     @pl.when(live)
     def _():

time: 58.4 us -> 58.4 us (level)
  no operation moved by 1% of the time
where the time goes in v8:
time: 58.4 us; the launch traced here: 58.2 us
  blocking collectives  51.8 us (89%)
  Pallas kernels  6.41 us (11%)
    all_to_all x2, blocking collectives, exchanged(): lax.all_to_all(array, ('sess', 'tp'), split_axis=0, concat_axis=0, tiled=...  51.8 us
    pallas_call x1, Pallas kernels, body(): pl.pallas_call(functools.partial(attend_kernel, owners, cap, pieces), out...  4.03 us
    pallas_call x1, Pallas kernels, body(): pl.pallas_call(functools.partial(dispatch_kernel, owners, cap), out_shape...  1.72 us

profile of v8, /device:TPU:1, one launch (start us, length us, event | category | flops | bytes accessed | tf_op | source)
XLA Modules:
  0.0 58.2 jit_solution(16404677560645098819)
XLA Ops:
  0.0 0.0 copy-start
  0.0 1.7 %dispatch.1 = (bf16[1024,128]{1,0:T(8,128)(2,1)}, bf16[32,32]{1,0:T(8,128)(2,1)S(1)}, f32[32,128]{1,0:T(8,128)S(1)}, s32[1,128]{1,0:T(1,128)S(1)}, f32[32,128]{1...) custom-call(s32[256]{0:T(256)} %session_hbm.1, s32[256]{0:T(256)} %owner_hbm.1, ...), custom_call_target="tpu_custom_call" | custom-call | flops 1000000000 | bytes 10000000 | tf_op jit(solution)/shard_map/dispatch/pallas_call | solution.py:384
  1.7 31.4 %all_to_all.22 = bf16[256,4,128]{2,1,0:T(4,128)(2,1)S(1)} all-to-all(bf16[256,4,128]{2,1,0:T(4,128)(2,1)} %bitcast.13), channel_id=1, replica_groups=mesh['sess'=16,'tp'=16] {'sess','tp'}, dimensions={0} | all-to-all | bytes 524288 | tf_op jit(solution)/shard_map/all_to_all | solution.py:369
  33.1 0.0 copy-done
  33.1 4.0 %attend.1 = bf16[1024,128]{1,0:T(8,128)(2,1)S(1)} custom-call(bf16[1024,128]{1,0:T(8,128)(2,1)S(1)} %bitcast.9, bf16[3,4096,128]{2,1,0:T(8,128)(2,1)S(1)} %copy-done, bf16[32,32]{1,0:T(8,128)(2,1)S(1)} %get-tuple-element.13.collect_ref, f32[32,128]{1,0:T(8,128)S(1)} %get-tuple-element.14.place_ref, s32[1,128]{1,0:T(1,128)S(1)} %get-tuple-element.15.length_ref, ...), custom_call_target="tpu_custom_call" | custom-call | tf_op jit(solution)/shard_map/attend/pallas_call | solution.py:415
  37.1 20.4 %all_to_all.23 = bf16[256,4,128]{2,1,0:T(4,128)(2,1)S(1)} all-to-all(bf16[256,4,128]{2,1,0:T(4,128)(2,1)S(1)} %bitcast.10), channel_id=1, replica_groups=mesh['sess'=16,'tp'=16] {'sess','tp'}, dimensions={0} | all-to-all | bytes 524288 | tf_op jit(solution)/shard_map/all_to_all | solution.py:369
  57.5 0.7 %finish.1 = bf16[16,256]{1,0:T(8,128)(2,1)} custom-call(bf16[1024,128]{1,0:T(8,128)(2,1)S(1)} %bitcast.11, bf16[16,256]{1,0:T(8,128)(2,1)S(1)} %get-tuple-element.17.frames_ref, s32[16,128]{1,0:T(8,128)S(1)} %get-tuple-element.18.target_ref), custom_call_target="tpu_custom_call" | custom-call | tf_op jit(solution)/shard_map/finish/pallas_call | solution.py:427
Async XLA Ops:
  0.0 33.1 %copy-start = (bf16[3,4096,128]{2,1,0:T(8,128)(2,1)S(1)}, bf16[3,4096,128]{2,1,0:T(8,128)(2,1)}, u32[]{:S(2)}) copy-start(bf16[3,4096,128]{2,1,0:T(8,128)(2,1)} %w_ref.1) | copy-start | bytes 9437188
